TPU v7x, 32 devices: a whole 2x2x4 slice. The times are simulated.
32 devices in a mesh: rep: 4 (over y, x), fsdp: 4 (over z), ctx: 2 (over core).
Axes of the slice: x: 2, y: 2, z: 4, core: 2. Of those that a mesh axis runs over, the one named last changes fastest.
Arguments:
- inputs: bfloat16 [2, 16, 1024, 768], P(None, ('rep', 'fsdp'), 'ctx'), may hold values from -6 to 6
- weight_qkv: bfloat16 [768, 2304], P('fsdp'), may hold values from -0.21875 to 0.21875
- bias_query: bfloat16 [768], P('fsdp'), may hold values from -3 to 3
- bias_value: bfloat16 [768], P('fsdp'), may hold values from -3 to 3
- weight_mix: bfloat16 [768, 768], P('fsdp'), may hold values from -1.75 to 1.75
- bias_mix: bfloat16 [768], P('fsdp'), may hold values from -2 to 2
- gain_attn: bfloat16 [768], P('fsdp'), may hold values from 0.099609375 to 1.8984375
- shift_attn: bfloat16 [768], P('fsdp'), may hold values from -2 to 2
- gain_mlp: bfloat16 [768], P('fsdp'), may hold values from 0.099609375 to 1.8984375
- shift_mlp: bfloat16 [768], P('fsdp'), may hold values from -2 to 2
- weight_up: bfloat16 [768, 3072], P('fsdp'), may hold values from -0.21875 to 0.21875
- bias_up: bfloat16 [3072], P('fsdp'), may hold values from -3 to 3
- weight_down: bfloat16 [3072, 768], P('fsdp'), may hold values from -0.109375 to 0.109375
- bias_down: bfloat16 [768], P('fsdp'), may hold values from -2 to 2
- cotangent: bfloat16 [2, 16, 1024, 768], P(None, ('rep', 'fsdp'), 'ctx'), may hold values from -6 to 6
Outputs:
- outputs: bfloat16 [2, 16, 1024, 768], P(None, ('rep', 'fsdp'), 'ctx')
- grad_inputs: float32 [2, 16, 1024, 768], P(None, ('rep', 'fsdp'), 'ctx')
- weight_qkv_grad: float32 [768, 2304], P('fsdp')
- bias_query_grad: float32 [768], P('fsdp')
- bias_value_grad: float32 [768], P('fsdp')
- weight_mix_grad: float32 [768, 768], P('fsdp')
- bias_mix_grad: float32 [768], P('fsdp')
- gain_attn_grad: float32 [768], P('fsdp')
- shift_attn_grad: float32 [768], P('fsdp')
- gain_mlp_grad: float32 [768], P('fsdp')
- shift_mlp_grad: float32 [768], P('fsdp')
- weight_up_grad: float32 [768, 3072], P('fsdp')
- bias_up_grad: float32 [3072], P('fsdp')
- weight_down_grad: float32 [3072, 768], P('fsdp')
- bias_down_grad: float32 [768], P('fsdp')
All inputs are finite; a program needn't handle non-finite values.
Results may differ from a plain program's by a relative error of at most 0.018.
Values may be sent and summed in bfloat16 or wider, within the bound.
A program may use at most 320 MiB of HBM per device.

v0:
```python
from functools import partial

import jax
import jax.numpy as jnp
from jax import lax
from jax.sharding import PartitionSpec as P

H = 12


EPS = 1e-05


def from_behind(x, axis, by):
    peers = lax.axis_size(axis)
    pairs = [(i, i + by) for i in range(peers) if 0 <= i + by < peers]
    return lax.ppermute(x, axis, pairs)


def for_sending(x):

    def short(part):
        return part.astype(jnp.bfloat16) if part.dtype == jnp.float32 else part

    return jax.tree.map(short, x)


def norm_stats(values):
    center = values - jnp.mean(values, axis=-1, keepdims=True)
    inverse = lax.rsqrt(jnp.mean(center * center, axis=-1, keepdims=True) + EPS)
    return (center * inverse, inverse)


def norm_back(grad_norm, normal, inverse, gain):
    scaled = grad_norm * gain
    return inverse * (
        scaled
        - jnp.mean(scaled, axis=-1, keepdims=True)
        - normal * jnp.mean(scaled * normal, axis=-1, keepdims=True)
    )


def column_sum(values):
    return jnp.sum(values.astype(jnp.float32), axis=(0, 1))


def outer_sum(left, right):
    return jnp.einsum("sri,srj->ij", left, right, preferred_element_type=jnp.float32)


def project(left, weight):
    return jnp.einsum("sri,ij->srj", left, weight, preferred_element_type=jnp.float32)


def project_back(grad_rows, weight):
    return jnp.einsum("srj,ij->sri", grad_rows, weight, preferred_element_type=jnp.float32)


def split_heads(values):
    return values.reshape(values.shape[0], values.shape[1], H, values.shape[2] // H)


def attention_scores(query_heads, key_heads, allowed, factor):
    raw = jnp.einsum("sqhd,skhd->shqk", query_heads, key_heads, preferred_element_type=jnp.float32)
    return jnp.where(allowed, raw * factor, -1e30)


def local(
    inputs,
    weight_qkv,
    bias_query,
    bias_value,
    weight_mix,
    bias_mix,
    gain_attn,
    shift_attn,
    gain_mlp,
    shift_mlp,
    weight_up,
    bias_up,
    weight_down,
    bias_down,
    cotangent,
):
    shards = (
        weight_qkv,
        bias_query,
        bias_value,
        weight_mix,
        bias_mix,
        gain_attn,
        shift_attn,
        gain_mlp,
        shift_mlp,
        weight_up,
        bias_up,
        weight_down,
        bias_down,
    )
    width = weight_qkv.shape[1] // 3
    factor = (width // H) ** (-0.5)
    rows = inputs.shape[2]
    owners = lax.axis_size("fsdp")
    ctx_index = lax.axis_index("ctx")
    query_pos = lax.broadcasted_iota(jnp.int32, (rows, 2 * rows), 0)
    key_pos = lax.broadcasted_iota(jnp.int32, (rows, 2 * rows), 1) - rows
    allowed = (key_pos <= query_pos) & ((key_pos >= 0) | (ctx_index > 0))
    whole_zeros = tuple(
        (jnp.zeros((item.shape[0] * owners,) + item.shape[1:], jnp.float32) for item in shards)
    )
    bf16 = jnp.bfloat16
    f32 = jnp.float32

    def micro(totals, pair):
        tokens_in, grad_in = pair
        full = (
            lax.all_gather(shards[0], "fsdp", axis=0, tiled=True),
            lax.all_gather(shards[1], "fsdp", axis=0, tiled=True),
            lax.all_gather(shards[2], "fsdp", axis=0, tiled=True),
            lax.all_gather(shards[3], "fsdp", axis=0, tiled=True),
            lax.all_gather(shards[4], "fsdp", axis=0, tiled=True),
            lax.all_gather(shards[5], "fsdp", axis=0, tiled=True),
            lax.all_gather(shards[6], "fsdp", axis=0, tiled=True),
            lax.all_gather(shards[7], "fsdp", axis=0, tiled=True),
            lax.all_gather(shards[8], "fsdp", axis=0, tiled=True),
            lax.all_gather(shards[9], "fsdp", axis=0, tiled=True),
            lax.all_gather(shards[10], "fsdp", axis=0, tiled=True),
            lax.all_gather(shards[11], "fsdp", axis=0, tiled=True),
            lax.all_gather(shards[12], "fsdp", axis=0, tiled=True),
        )
        tokens = tokens_in.astype(f32)
        normal_one, inverse_one = norm_stats(tokens)
        first = (normal_one * full[5] + full[6]).astype(bf16)
        joined = project(first, full[0])
        query = (joined[..., :width] + full[1]).astype(bf16)
        key_own = joined[..., width : 2 * width].astype(bf16)
        value_own = (joined[..., 2 * width :] + full[2]).astype(bf16)
        key_prev, value_prev = from_behind((key_own, value_own), "ctx", 1)
        key_heads = split_heads(jnp.concatenate([key_prev, key_own], axis=1))
        value_heads = split_heads(jnp.concatenate([value_prev, value_own], axis=1))
        query_heads = split_heads(query)
        scores = attention_scores(query_heads, key_heads, allowed, factor)
        top = jnp.max(scores, axis=-1, keepdims=True)
        logsum = top + jnp.log(jnp.sum(jnp.exp(scores - top), axis=-1, keepdims=True))
        probs_low = jnp.exp(scores - logsum).astype(bf16)
        mixed = jnp.einsum("shqk,skhd->sqhd", probs_low, value_heads, preferred_element_type=f32)
        mixed = mixed.reshape(tokens.shape).astype(bf16)
        middle = tokens + project(mixed, full[3]) + full[4]
        normal_two, inverse_two = norm_stats(middle)
        second = (normal_two * full[7] + full[8]).astype(bf16)
        before = project(second, full[9]) + full[10]
        active = jax.nn.gelu(before, approximate=True).astype(bf16)
        result = (middle + project(active, full[11]) + full[12]).astype(bf16)
        again = (
            lax.all_gather(shards[0], "fsdp", axis=0, tiled=True),
            lax.all_gather(shards[1], "fsdp", axis=0, tiled=True),
            lax.all_gather(shards[2], "fsdp", axis=0, tiled=True),
            lax.all_gather(shards[3], "fsdp", axis=0, tiled=True),
            lax.all_gather(shards[4], "fsdp", axis=0, tiled=True),
            lax.all_gather(shards[5], "fsdp", axis=0, tiled=True),
            lax.all_gather(shards[6], "fsdp", axis=0, tiled=True),
            lax.all_gather(shards[7], "fsdp", axis=0, tiled=True),
            lax.all_gather(shards[8], "fsdp", axis=0, tiled=True),
            lax.all_gather(shards[9], "fsdp", axis=0, tiled=True),
            lax.all_gather(shards[10], "fsdp", axis=0, tiled=True),
            lax.all_gather(shards[11], "fsdp", axis=0, tiled=True),
            lax.all_gather(shards[12], "fsdp", axis=0, tiled=True),
        )
        grad_out = grad_in.astype(f32)
        d_down = grad_out.astype(bf16)
        g_wdown = outer_sum(active, d_down)
        g_bdown = column_sum(d_down)
        d_active = project_back(d_down, again[11])
        gelu_back = jax.vjp(partial(jax.nn.gelu, approximate=True), before)[1]
        d_before = gelu_back(d_active)[0].astype(bf16)
        g_wup = outer_sum(second, d_before)
        g_bup = column_sum(d_before)
        d_second = project_back(d_before, again[9])
        g_gmlp = jnp.sum(d_second * normal_two, axis=(0, 1))
        g_smlp = jnp.sum(d_second, axis=(0, 1))
        d_middle = grad_out + norm_back(d_second, normal_two, inverse_two, again[7])
        d_branch = d_middle.astype(bf16)
        g_wmix = outer_sum(mixed, d_branch)
        g_bmix = column_sum(d_branch)
        d_mixed = split_heads(project_back(d_branch, again[3]).astype(bf16))
        scores = attention_scores(query_heads, key_heads, allowed, factor)
        probs = jnp.exp(scores - logsum)
        probs_low = probs.astype(bf16)
        d_probs = jnp.einsum("sqhd,skhd->shqk", d_mixed, value_heads, preferred_element_type=f32)
        d_scores = (
            probs * (d_probs - jnp.sum(d_probs * probs, axis=-1, keepdims=True)) * factor
        ).astype(bf16)
        d_query = jnp.einsum("shqk,skhd->sqhd", d_scores, key_heads, preferred_element_type=f32)
        d_query = d_query.reshape(tokens.shape).astype(bf16)
        d_key_all = jnp.einsum("shqk,sqhd->skhd", d_scores, query_heads, preferred_element_type=f32)
        d_value_all = jnp.einsum("shqk,sqhd->skhd", probs_low, d_mixed, preferred_element_type=f32)
        d_key_all = d_key_all.reshape(tokens.shape[0], 2 * rows, width)
        d_value_all = d_value_all.reshape(tokens.shape[0], 2 * rows, width)
        key_back, value_back = (
            from_behind(d_key_all[:, :rows].astype(jnp.bfloat16), "ctx", -1).astype(jnp.float32),
            from_behind(d_value_all[:, :rows].astype(jnp.bfloat16), "ctx", -1).astype(jnp.float32),
        )
        d_key = (d_key_all[:, rows:] + key_back).astype(bf16)
        d_value = (d_value_all[:, rows:] + value_back).astype(bf16)
        d_joined = jnp.concatenate([d_query, d_key, d_value], axis=-1)
        g_wqkv = outer_sum(first, d_joined)
        g_bquery = column_sum(d_query)
        g_bvalue = column_sum(d_value)
        d_first = project_back(d_joined, again[0])
        g_gattn = jnp.sum(d_first * normal_one, axis=(0, 1))
        g_sattn = jnp.sum(d_first, axis=(0, 1))
        d_tokens = d_middle + norm_back(d_first, normal_one, inverse_one, again[5])
        terms = (
            g_wqkv,
            g_bquery,
            g_bvalue,
            g_wmix,
            g_bmix,
            g_gattn,
            g_sattn,
            g_gmlp,
            g_smlp,
            g_wup,
            g_bup,
            g_wdown,
            g_bdown,
        )
        totals = tuple((left + right for left, right in zip(totals, terms)))
        return (totals, (result, d_tokens))

    totals, (results, grad_tokens) = lax.scan(micro, whole_zeros, (inputs, cotangent))
    shares = jax.tree.map(
        lambda part: part.astype(jnp.float32),
        lax.psum_scatter(for_sending(totals), "fsdp", scatter_dimension=0, tiled=True),
    )
    summed = jax.tree.map(
        lambda part: part.astype(jnp.float32), lax.psum(for_sending(shares), ("rep", "ctx"))
    )
    return (results, grad_tokens) + tuple(summed)


def solution(mesh):
    in_specs = (
        P(None, ("rep", "fsdp"), "ctx", None),
        P("fsdp", None),
        P("fsdp"),
        P("fsdp"),
        P("fsdp", None),
        P("fsdp"),
        P("fsdp"),
        P("fsdp"),
        P("fsdp"),
        P("fsdp"),
        P("fsdp", None),
        P("fsdp"),
        P("fsdp", None),
        P("fsdp"),
        P(None, ("rep", "fsdp"), "ctx", None),
    )
    out_specs = (
        P(None, ("rep", "fsdp"), "ctx", None),
        P(None, ("rep", "fsdp"), "ctx", None),
        P("fsdp", None),
        P("fsdp"),
        P("fsdp"),
        P("fsdp", None),
        P("fsdp"),
        P("fsdp"),
        P("fsdp"),
        P("fsdp"),
        P("fsdp"),
        P("fsdp", None),
        P("fsdp"),
        P("fsdp", None),
        P("fsdp"),
    )
    return jax.shard_map(local, mesh=mesh, in_specs=in_specs, out_specs=out_specs, check_vma=False)
```

profile of v0, /device:TPU:1, one launch (start us, length us, event | category | flops | bytes accessed | tf_op | source)
XLA Modules:
  0.0 1351.9 jit_solution(5778753269937234375)
XLA Ops:
  8.2 976.6 %while.41 = (s32[]{:T(128)}, f32[768,2304]{1,0:T(8,128)}, f32[768]{0:T(1024)}, f32[768]{0:T(1024)}, f32[768,768]{1,0:T(8,128)}, /*index=5*/f32[768]{0:T(1024)}, ...) while((s32[]{:T(128)}, f32[768,2304]{1,0:T(8,128)}, ...), condition=%wide.region_21.22_spmd.clone, body=%wide.region_0.21_spmd.clone.sunk | while | flops 26950144000 | bytes 699213696 | solution.py:231
  19.4 17.9 %all-reduce.30 = (bf16[768]{0:T(1024)(128)(2,1)S(1)}, bf16[768]{0:T(1024)(128)(2,1)S(1)}, bf16[768]{0:T(1024)(128)(2,1)S(1)}, bf16[768]{0:T(1024)(128)(2,1)S(1)}...) all-reduce(bf16[768]{0:T(1024)(128)(2,1)S(1)} %dynamic-update-slice, ...), channel_id=1, replica_groups=mesh['rep'=4,'fsdp'=4,'ctx'=2] {'fsdp'}, use_global_device_ids=true, to_apply=%add.1 | all-reduce | flops 6144 | bytes 24576 | tf_op jit(solution)/shard_map/while
  39.1 44.4 %all-gather.11.cloned.1.call-done = bf16[768,2304]{1,0:T(8,128)(2,1)} async-done(((bf16[192,2304]{1,0:T(8,128)(2,1)}), bf16[768,2304]{1,0:T(8,128)(2,1)}) %all-gather.11.cloned.1.call-update) | async-done | bytes 3538960 | tf_op jit(solution)/shard_map/while/body/eval_jaxpr/all_gather | solution.py:117
  83.5 4.1 convolution_bitcast_fusion.2
  91.7 10.4 all-gather.3
  110.8 15.6 %fusion.201 = (f32[12,512]{1,0:T(8,128)S(1)}, f32[12,512,1024]{2,1,0:T(8,128)}) fusion(pred[512,1024]{1,0:T(8,128)(4,1)} %fusion.200, bf16[512,12,64]{0,2,1:T(8,128)(2,1)} %bitcast.212, bf16[1024,12,64]{0,2,1:T(8,128)(2,1)} %bitcast.210), kind=kOutput, calls=%fused_computation.8.clone.1 | convolution fusion | flops 824174592 | bytes 28073984 | tf_op jit(solution)/shard_map/while/body/eval_jaxpr/sqhd,skhd->shqk/dot_general | solution.py:64
  126.4 11.8 exponential_reduce_fusion.2
  138.3 12.1 convolution_convert_fusion.4
  153.3 51.2 %all-gather.13.cloned.1.call-done = bf16[768,3072]{1,0:T(8,128)(2,1)} async-done(((bf16[192,3072]{1,0:T(8,128)(2,1)}), bf16[768,3072]{1,0:T(8,128)(2,1)}) %all-gather.13.cloned.1.call-update) | async-done | bytes 4718608 | tf_op jit(solution)/shard_map/while/body/eval_jaxpr/all_gather | solution.py:126
  204.5 7.1 fusion.203
  211.6 82.2 %all-gather.15.cloned.1.call-done = bf16[3072,768]{1,0:T(8,128)(2,1)} async-done(((bf16[768,768]{1,0:T(8,128)(2,1)}), bf16[3072,768]{1,0:T(8,128)(2,1)}) %all-gather.15.cloned.1.call-update) | async-done | bytes 4718608 | tf_op jit(solution)/shard_map/while/body/eval_jaxpr/all_gather | solution.py:166
  293.8 9.8 convert_reduce_fusion.13
  312.1 13.6 %fusion.204 = f32[12,64,1024]{2,1,0:T(8,128)} fusion(bf16[512,12,64]{0,2,1:T(8,128)(2,1)} %bitcast.208, f32[12,512]{1,0:T(8,128)S(1)} %log_add_fusion.2, f32[12,512,1024]{2,1,0:T(8,128)} %get-tuple-element.914, pred[512,1024]{1,0:T(8,128)(4,1)} %fusion.200), kind=kOutput, calls=%fused_computation.107.clone.1 | convolution fusion | flops 830472192 | bytes 29646848 | tf_op jit(solution)/shard_map/while/body/eval_jaxpr/shqk,sqhd->skhd/dot_general | solution.py:196
  325.7 10.1 fusion.205
  335.8 52.3 %convert_reduce_fusion.16 = (f32[12,64]{1,0:T(8,128)S(1)}, bf16[12,64,512]{2,1,0:T(8,128)(2,1)}) fusion(bf16[1024,12,64]{0,2,1:T(8,128)(2,1)} %bitcast.211, f32[12,512,1024]{2,1,0:T(8,128)} %fusion.205, f32[12,512]{1,0:T(8,128)S(1)} %log_add_fusion.2, f32[12,512,1024]{2,1,0:T(8,128)} %get-tuple-element.914, pred[512,1024]{1,0:T(8,128)(4,1)} %fusion.200), kind=kOutput, calls=%fused_computation.77.clone.1 | convolution fusion | flops 875698432 | bytes 53242880 | tf_op jit(solution)/shard_map/while/body/eval_jaxpr/shqk,skhd->sqhd/dot_general | solution.py:193
  388.1 54.1 %fusion.206 = f32[12,64,1024]{2,1,0:T(8,128)} fusion(bf16[512,12,64]{0,2,1:T(8,128)(2,1)} %bitcast.213, f32[12,512,1024]{2,1,0:T(8,128)} %fusion.205, f32[12,512]{1,0:T(8,128)S(1)} %log_add_fusion.2, f32[12,512,1024]{2,1,0:T(8,128)} %get-tuple-element.914, pred[512,1024]{1,0:T(8,128)(4,1)} %fusion.200), kind=kOutput, calls=%fused_computation.10.clone.1 | convolution fusion | flops 874519552 | bytes 54812672 | tf_op jit(solution)/shard_map/while/body/eval_jaxpr/shqk,sqhd->skhd/dot_general | solution.py:195
  442.1 10.5 select_add_fusion.31
  458.4 5.5 select_add_fusion.29
  466.9 9.1 fusion.209
  481.1 7.4 select_add_fusion.23
  504.7 13.6 %all-reduce.30 = (bf16[768]{0:T(1024)(128)(2,1)S(1)}, bf16[768]{0:T(1024)(128)(2,1)S(1)}, bf16[768]{0:T(1024)(128)(2,1)S(1)}, bf16[768]{0:T(1024)(128)(2,1)S(1)}...) all-reduce(bf16[768]{0:T(1024)(128)(2,1)S(1)} %dynamic-update-slice, ...), channel_id=1, replica_groups=mesh['rep'=4,'fsdp'=4,'ctx'=2] {'fsdp'}, use_global_device_ids=true, to_apply=%add.1 | all-reduce | flops 6144 | bytes 24576 | tf_op jit(solution)/shard_map/while
  520.0 44.5 %all-gather.11.cloned.1.call-done = bf16[768,2304]{1,0:T(8,128)(2,1)} async-done(((bf16[192,2304]{1,0:T(8,128)(2,1)}), bf16[768,2304]{1,0:T(8,128)(2,1)}) %all-gather.11.cloned.1.call-update) | async-done | bytes 3538960 | tf_op jit(solution)/shard_map/while/body/eval_jaxpr/all_gather | solution.py:117
  572.8 10.4 all-gather.3
  591.6 15.6 %fusion.201 = (f32[12,512]{1,0:T(8,128)S(1)}, f32[12,512,1024]{2,1,0:T(8,128)}) fusion(pred[512,1024]{1,0:T(8,128)(4,1)} %fusion.200, bf16[512,12,64]{0,2,1:T(8,128)(2,1)} %bitcast.212, bf16[1024,12,64]{0,2,1:T(8,128)(2,1)} %bitcast.210), kind=kOutput, calls=%fused_computation.8.clone.1 | convolution fusion | flops 824174592 | bytes 28073984 | tf_op jit(solution)/shard_map/while/body/eval_jaxpr/sqhd,skhd->shqk/dot_general | solution.py:64
  607.3 11.8 exponential_reduce_fusion.2
  619.1 12.1 convolution_convert_fusion.4
  634.2 51.3 %all-gather.13.cloned.1.call-done = bf16[768,3072]{1,0:T(8,128)(2,1)} async-done(((bf16[192,3072]{1,0:T(8,128)(2,1)}), bf16[768,3072]{1,0:T(8,128)(2,1)}) %all-gather.13.cloned.1.call-update) | async-done | bytes 4718608 | tf_op jit(solution)/shard_map/while/body/eval_jaxpr/all_gather | solution.py:126
  685.5 7.1 fusion.203
  692.6 82.4 %all-gather.15.cloned.1.call-done = bf16[3072,768]{1,0:T(8,128)(2,1)} async-done(((bf16[768,768]{1,0:T(8,128)(2,1)}), bf16[3072,768]{1,0:T(8,128)(2,1)}) %all-gather.15.cloned.1.call-update) | async-done | bytes 4718608 | tf_op jit(solution)/shard_map/while/body/eval_jaxpr/all_gather | solution.py:166
  775.0 9.3 convert_reduce_fusion.13
  792.7 13.6 %fusion.204 = f32[12,64,1024]{2,1,0:T(8,128)} fusion(bf16[512,12,64]{0,2,1:T(8,128)(2,1)} %bitcast.208, f32[12,512]{1,0:T(8,128)S(1)} %log_add_fusion.2, f32[12,512,1024]{2,1,0:T(8,128)} %get-tuple-element.914, pred[512,1024]{1,0:T(8,128)(4,1)} %fusion.200), kind=kOutput, calls=%fused_computation.107.clone.1 | convolution fusion | flops 830472192 | bytes 29646848 | tf_op jit(solution)/shard_map/while/body/eval_jaxpr/shqk,sqhd->skhd/dot_general | solution.py:196
  806.4 10.1 fusion.205
  816.4 52.5 %convert_reduce_fusion.16 = (f32[12,64]{1,0:T(8,128)S(1)}, bf16[12,64,512]{2,1,0:T(8,128)(2,1)}) fusion(bf16[1024,12,64]{0,2,1:T(8,128)(2,1)} %bitcast.211, f32[12,512,1024]{2,1,0:T(8,128)} %fusion.205, f32[12,512]{1,0:T(8,128)S(1)} %log_add_fusion.2, f32[12,512,1024]{2,1,0:T(8,128)} %get-tuple-element.914, pred[512,1024]{1,0:T(8,128)(4,1)} %fusion.200), kind=kOutput, calls=%fused_computation.77.clone.1 | convolution fusion | flops 875698432 | bytes 53242880 | tf_op jit(solution)/shard_map/while/body/eval_jaxpr/shqk,skhd->sqhd/dot_general | solution.py:193
  869.0 54.0 %fusion.206 = f32[12,64,1024]{2,1,0:T(8,128)} fusion(bf16[512,12,64]{0,2,1:T(8,128)(2,1)} %bitcast.213, f32[12,512,1024]{2,1,0:T(8,128)} %fusion.205, f32[12,512]{1,0:T(8,128)S(1)} %log_add_fusion.2, f32[12,512,1024]{2,1,0:T(8,128)} %get-tuple-element.914, pred[512,1024]{1,0:T(8,128)(4,1)} %fusion.200), kind=kOutput, calls=%fused_computation.10.clone.1 | convolution fusion | flops 874519552 | bytes 54812672 | tf_op jit(solution)/shard_map/while/body/eval_jaxpr/shqk,sqhd->skhd/dot_general | solution.py:195
  923.0 13.3 select_add_fusion.31
  942.1 7.9 select_add_fusion.29
  952.9 9.1 fusion.209
  967.1 9.5 select_add_fusion.23
  987.8 5.2 convert_element_type.434
  993.0 6.5 convert_element_type.452
  999.6 6.4 convert_element_type.456
  1006.1 8.8 reduce-scatter.7.cloned.1.call-done
  1014.9 67.2 %reduce-scatter.5.cloned.1.call-done = bf16[192,2304]{1,0:T(8,128)(2,1)} async-done(((bf16[768,2304]{1,0:T(8,128)(2,1)}), bf16[192,2304]{1,0:T(8,128)(2,1)}) %reduce-scatter.5.cloned.1.call-update) | async-done | bytes 884752 | tf_op jit(solution)/shard_map/reduce_scatter | solution.py:234
  1082.1 87.9 %reduce-scatter.9.cloned.1.call-done = bf16[192,3072]{1,0:T(8,128)(2,1)} async-done(((bf16[768,3072]{1,0:T(8,128)(2,1)}), bf16[192,3072]{1,0:T(8,128)(2,1)}) %reduce-scatter.9.cloned.1.call-update) | async-done | bytes 1179664 | tf_op jit(solution)/shard_map/reduce_scatter | solution.py:234
  1170.0 88.1 %reduce-scatter.11.cloned.1.call-done = bf16[768,768]{1,0:T(8,128)(2,1)} async-done(((bf16[3072,768]{1,0:T(8,128)(2,1)}), bf16[768,768]{1,0:T(8,128)(2,1)}) %reduce-scatter.11.cloned.1.call-update) | async-done | bytes 1179664 | tf_op jit(solution)/shard_map/reduce_scatter | solution.py:234
  1260.1 14.7 %all-reduce.28 = (bf16[768]{0:T(1024)(128)(2,1)S(1)}, bf16[768]{0:T(1024)(128)(2,1)S(1)}, bf16[768]{0:T(1024)(128)(2,1)S(1)}, bf16[768]{0:T(1024)(128)(2,1)S(1)}...) all-reduce(bf16[768]{0:T(1024)(128)(2,1)S(1)} %convert_element_type, ...), channel_id=3, replica_groups=mesh['rep'=4,'fsdp'=4,'ctx'=2] {'fsdp'}, use_global_device_ids=true, to_apply=%region_24.25.clone | all-reduce | flops 9216 | bytes 36864
  1275.5 16.1 %all-reduce.26 = (bf16[192]{0:T(256)(128)(2,1)S(1)}, bf16[192]{0:T(256)(128)(2,1)S(1)}, bf16[192]{0:T(256)(128)(2,1)S(1)}, bf16[192]{0:T(256)(128)(2,1)S(1)}, bf...) all-reduce(bf16[192]{0:T(256)(128)(2,1)S(1)} %dynamic-slice.10, ...), channel_id=1, replica_groups=mesh['rep'=4,'fsdp'=4,'ctx'=2] {'rep','ctx'}, use_global_device_ids=true, to_apply=%region_25.26 | all-reduce | flops 2304 | bytes 9216 | tf_op jit(solution)/shard_map/psum | solution.py:237
  1296.7 39.6 %all-reduce.33.cloned.1.call-done = (bf16[192,2304]{1,0:T(8,128)(2,1)}, bf16[192,768]{1,0:T(8,128)(2,1)}, bf16[192,3072]{1,0:T(8,128)(2,1)}, bf16[768,768]{1,0:T(8,128)(2,1)}) async-done(((bf16[192,2304]{1,0:T(8,128)(2,1)}, bf16[192,768]{1,0:T(8,128)(2,1)}, bf16[192,3072]{1,0:T(8,128)(2,1)}, bf16[768,768]{1,0:T(8,128)(2,1)}), (bf16[192,2304]{1,0:T(8,128)(2,1)}, bf16[192,768]{1,0:T(8,128)(2,1)}, ...) | async-done | bytes 3538960 | tf_op jit(solution)/shard_map/psum | solution.py:237
  (409 shorter events, 129.6 us)
Async XLA Ops:
  8.5 93.8 %copy-start.21 = (s32[1024]{0:T(1024)}, s32[1024]{0:T(1024)S(1)}, u32[]{:S(2)}) copy-start(s32[1024]{0:T(1024)S(1)} %get-tuple-element.1055) | copy-start | bytes 12292 | tf_op jit(solution)/shard_map/while
  8.5 93.8 %copy-start.41 = (pred[1024]{0:T(1024)(128)(4,1)}, pred[1024]{0:T(1024)(128)(4,1)S(1)}, u32[]{:S(2)}) copy-start(pred[1024]{0:T(1024)(128)(4,1)S(1)} %get-tuple-element.1056) | copy-start | bytes 3076 | tf_op jit(solution)/shard_map/while
  8.5 30.2 %copy-start.4 = (bf16[2,1,512,768]{3,2,1,0:T(8,128)(2,1)S(1)}, bf16[2,1,512,768]{3,2,1,0:T(8,128)(2,1)}, u32[]{:S(2)}) copy-start(bf16[2,1,512,768]{3,2,1,0:T(8,128)(2,1)} %get-tuple-element.1040) | copy-start | bytes 4718596 | tf_op jit(solution)/shard_map/while
  8.5 75.0 %all-gather.11.cloned.1.call-start = ((), (), s32[]{:S(2)}) async-start(), calls=%async_computation.10 | async-start | bytes 4423680 | tf_op jit(solution)/shard_map/while/body/eval_jaxpr/all_gather | solution.py:117
  9.3 141.1 %all-gather.9.cloned.1.call-start = ((), (), s32[]{:S(2)}) async-start(), calls=%async_computation.9 | async-start | bytes 1474560 | tf_op jit(solution)/shard_map/while/body/eval_jaxpr/all_gather | solution.py:120
  10.0 194.5 %all-gather.13.cloned.1.call-start = ((), (), s32[]{:S(2)}) async-start(), calls=%async_computation.11 | async-start | bytes 5898240 | tf_op jit(solution)/shard_map/while/body/eval_jaxpr/all_gather | solution.py:126
  10.8 283.1 %all-gather.15.cloned.1.call-start = ((), (), s32[]{:S(2)}) async-start(), calls=%async_computation.12 | async-start | bytes 5898240 | tf_op jit(solution)/shard_map/while/body/eval_jaxpr/all_gather | solution.py:166
  87.6 14.5 %copy-start.12 = (bf16[2,1,512,768]{3,2,1,0:T(8,128)(2,1)S(1)}, bf16[2,1,512,768]{3,2,1,0:T(8,128)(2,1)}, u32[]{:S(2)}) copy-start(bf16[2,1,512,768]{3,2,1,0:T(8,128)(2,1)} %get-tuple-element.1045) | copy-start | bytes 4718596 | tf_op jit(solution)/shard_map/while
  88.0 16.7 %collective-permute-start = (bf16[1,512,768]{2,1,0:T(8,128)(2,1)S(1)}, bf16[1,512,768]{2,1,0:T(8,128)(2,1)}, u32[]{:S(2)}, u32[]{:S(2)}) collective-permute-start(bf16[1,512,768]{2,1,0:T(8,128)(2,1)S(1)} %get-tuple-element.911), channel_id=1, source_target_pairs={{0,1},{2,3},{4,5},{6,7},{8,9},{10,11},{12,13},{14,15},{16,17},{18,... | collective-permute-start | bytes 2359304 | tf_op jit(solution)/shard_map/while/body/eval_jaxpr/ppermute | solution.py:17
  90.4 16.7 %collective-permute-start.1 = (bf16[1,512,768]{2,1,0:T(8,128)(2,1)}, bf16[1,512,768]{2,1,0:T(8,128)(2,1)}, u32[]{:S(2)}, u32[]{:S(2)}) collective-permute-start(bf16[1,512,768]{2,1,0:T(8,128)(2,1)} %slice.85), channel_id=1, source_target_pairs={{0,1},{2,3},{4,5},{6,7},{8,9},{10,11},{12,13},{14,15},{16,17},{18,... | collective-permute-start | bytes 2359304 | tf_op jit(solution)/shard_map/while/body/eval_jaxpr/ppermute | solution.py:17
  107.1 31.2 %copy-start = (bf16[1,1024,768]{1,2,0:T(8,128)(2,1)}, bf16[1,1024,768]{1,2,0:T(8,128)(2,1)S(1)}, u32[]{:S(2)}) copy-start(bf16[1,1024,768]{1,2,0:T(8,128)(2,1)S(1)} %copy.50) | copy-start | bytes 4718596 | tf_op jit(solution)/shard_map/while
  110.8 15.6 %copy-start.3 = (pred[512,1024]{1,0:T(8,128)(4,1)S(1)}, pred[512,1024]{1,0:T(8,128)(4,1)}, u32[]{:S(2)}) copy-start(pred[512,1024]{1,0:T(8,128)(4,1)} %fusion.200) | copy-start | bytes 1572868 | tf_op jit(solution)/shard_map/while
  153.3 140.5 %copy-start.13 = (bf16[2,1,512,768]{3,2,1,0:T(8,128)(2,1)S(1)}, bf16[2,1,512,768]{3,2,1,0:T(8,128)(2,1)}, u32[]{:S(2)}) copy-start(bf16[2,1,512,768]{3,2,1,0:T(8,128)(2,1)} %get-tuple-element.1045) | copy-start | bytes 4718596 | tf_op jit(solution)/shard_map/while
  312.1 13.6 %copy-start.1 = (bf16[1,1024,768]{1,2,0:T(8,128)(2,1)S(1)}, bf16[1,1024,768]{1,2,0:T(8,128)(2,1)}, u32[]{:S(2)}) copy-start(bf16[1,1024,768]{1,2,0:T(8,128)(2,1)} %copy-done) | copy-start | bytes 4718596 | tf_op jit(solution)/shard_map/while
  312.1 13.6 %copy-start.2 = (bf16[512,768]{0,1:T(8,128)(2,1)S(1)}, bf16[512,768]{0,1:T(8,128)(2,1)}, u32[]{:S(2)}) copy-start(bf16[512,768]{0,1:T(8,128)(2,1)} %copy.53) | copy-start | bytes 2359300 | tf_op jit(solution)/shard_map/while
  442.1 16.3 %copy-start.9 = (bf16[512,3072]{1,0:T(8,128)(2,1)S(1)}, bf16[512,3072]{1,0:T(8,128)(2,1)}, u32[]{:S(2)}) copy-start(bf16[512,3072]{1,0:T(8,128)(2,1)} %copy-done.8) | copy-start | bytes 9437188 | tf_op jit(solution)/shard_map/while
  455.0 22.6 %collective-permute-start.2 = (bf16[1,512,768]{1,2,0:T(8,128)(2,1)}, bf16[1,512,768]{1,2,0:T(8,128)(2,1)}, u32[]{:S(2)}, u32[]{:S(2)}) collective-permute-start(bf16[1,512,768]{1,2,0:T(8,128)(2,1)} %slice.86), channel_id=1, source_target_pairs={{1,0},{3,2},{5,4},{7,6},{9,8},{11,10},{13,12},{15,14},{17,16},{19,... | collective-permute-start | bytes 2359304 | tf_op jit(solution)/shard_map/while/body/eval_jaxpr/ppermute | solution.py:17
  465.5 15.0 %collective-permute-start.3 = (bf16[1,512,768]{1,2,0:T(8,128)(2,1)S(1)}, bf16[1,512,768]{1,2,0:T(8,128)(2,1)S(1)}, u32[]{:S(2)}, u32[]{:S(2)}) collective-permute-start(bf16[1,512,768]{1,2,0:T(8,128)(2,1)S(1)} %slice.87), channel_id=1, source_target_pairs={{1,0},{3,2},{5,4},{7,6},{9,8},{11,10},{13,12},{15,14},{17,16},{19,... | collective-permute-start | bytes 2359304 | tf_op jit(solution)/shard_map/while/body/eval_jaxpr/ppermute | solution.py:17
  494.0 89.3 %copy-start.21 = (s32[1024]{0:T(1024)}, s32[1024]{0:T(1024)S(1)}, u32[]{:S(2)}) copy-start(s32[1024]{0:T(1024)S(1)} %get-tuple-element.1055) | copy-start | bytes 12292 | tf_op jit(solution)/shard_map/while
  494.0 89.3 %copy-start.41 = (pred[1024]{0:T(1024)(128)(4,1)}, pred[1024]{0:T(1024)(128)(4,1)S(1)}, u32[]{:S(2)}) copy-start(pred[1024]{0:T(1024)(128)(4,1)S(1)} %get-tuple-element.1056) | copy-start | bytes 3076 | tf_op jit(solution)/shard_map/while
  494.0 25.6 %copy-start.4 = (bf16[2,1,512,768]{3,2,1,0:T(8,128)(2,1)S(1)}, bf16[2,1,512,768]{3,2,1,0:T(8,128)(2,1)}, u32[]{:S(2)}) copy-start(bf16[2,1,512,768]{3,2,1,0:T(8,128)(2,1)} %get-tuple-element.1040) | copy-start | bytes 4718596 | tf_op jit(solution)/shard_map/while
  494.1 70.5 %all-gather.11.cloned.1.call-start = ((), (), s32[]{:S(2)}) async-start(), calls=%async_computation.10 | async-start | bytes 4423680 | tf_op jit(solution)/shard_map/while/body/eval_jaxpr/all_gather | solution.py:117
  494.7 136.5 %all-gather.9.cloned.1.call-start = ((), (), s32[]{:S(2)}) async-start(), calls=%async_computation.9 | async-start | bytes 1474560 | tf_op jit(solution)/shard_map/while/body/eval_jaxpr/all_gather | solution.py:120
  495.2 190.3 %all-gather.13.cloned.1.call-start = ((), (), s32[]{:S(2)}) async-start(), calls=%async_computation.11 | async-start | bytes 5898240 | tf_op jit(solution)/shard_map/while/body/eval_jaxpr/all_gather | solution.py:126
  496.0 279.0 %all-gather.15.cloned.1.call-start = ((), (), s32[]{:S(2)}) async-start(), calls=%async_computation.12 | async-start | bytes 5898240 | tf_op jit(solution)/shard_map/while/body/eval_jaxpr/all_gather | solution.py:166
  568.7 14.5 %copy-start.12 = (bf16[2,1,512,768]{3,2,1,0:T(8,128)(2,1)S(1)}, bf16[2,1,512,768]{3,2,1,0:T(8,128)(2,1)}, u32[]{:S(2)}) copy-start(bf16[2,1,512,768]{3,2,1,0:T(8,128)(2,1)} %get-tuple-element.1045) | copy-start | bytes 4718596 | tf_op jit(solution)/shard_map/while
  569.0 16.7 %collective-permute-start = (bf16[1,512,768]{2,1,0:T(8,128)(2,1)S(1)}, bf16[1,512,768]{2,1,0:T(8,128)(2,1)}, u32[]{:S(2)}, u32[]{:S(2)}) collective-permute-start(bf16[1,512,768]{2,1,0:T(8,128)(2,1)S(1)} %get-tuple-element.911), channel_id=1, source_target_pairs={{0,1},{2,3},{4,5},{6,7},{8,9},{10,11},{12,13},{14,15},{16,17},{18,... | collective-permute-start | bytes 2359304 | tf_op jit(solution)/shard_map/while/body/eval_jaxpr/ppermute | solution.py:17
  571.4 16.6 %collective-permute-start.1 = (bf16[1,512,768]{2,1,0:T(8,128)(2,1)}, bf16[1,512,768]{2,1,0:T(8,128)(2,1)}, u32[]{:S(2)}, u32[]{:S(2)}) collective-permute-start(bf16[1,512,768]{2,1,0:T(8,128)(2,1)} %slice.85), channel_id=1, source_target_pairs={{0,1},{2,3},{4,5},{6,7},{8,9},{10,11},{12,13},{14,15},{16,17},{18,... | collective-permute-start | bytes 2359304 | tf_op jit(solution)/shard_map/while/body/eval_jaxpr/ppermute | solution.py:17
  587.9 31.2 %copy-start = (bf16[1,1024,768]{1,2,0:T(8,128)(2,1)}, bf16[1,1024,768]{1,2,0:T(8,128)(2,1)S(1)}, u32[]{:S(2)}) copy-start(bf16[1,1024,768]{1,2,0:T(8,128)(2,1)S(1)} %copy.50) | copy-start | bytes 4718596 | tf_op jit(solution)/shard_map/while
  591.6 15.6 %copy-start.3 = (pred[512,1024]{1,0:T(8,128)(4,1)S(1)}, pred[512,1024]{1,0:T(8,128)(4,1)}, u32[]{:S(2)}) copy-start(pred[512,1024]{1,0:T(8,128)(4,1)} %fusion.200) | copy-start | bytes 1572868 | tf_op jit(solution)/shard_map/while
  634.2 140.8 %copy-start.13 = (bf16[2,1,512,768]{3,2,1,0:T(8,128)(2,1)S(1)}, bf16[2,1,512,768]{3,2,1,0:T(8,128)(2,1)}, u32[]{:S(2)}) copy-start(bf16[2,1,512,768]{3,2,1,0:T(8,128)(2,1)} %get-tuple-element.1045) | copy-start | bytes 4718596 | tf_op jit(solution)/shard_map/while
  792.7 13.6 %copy-start.1 = (bf16[1,1024,768]{1,2,0:T(8,128)(2,1)S(1)}, bf16[1,1024,768]{1,2,0:T(8,128)(2,1)}, u32[]{:S(2)}) copy-start(bf16[1,1024,768]{1,2,0:T(8,128)(2,1)} %copy-done) | copy-start | bytes 4718596 | tf_op jit(solution)/shard_map/while
  792.7 13.6 %copy-start.2 = (bf16[512,768]{0,1:T(8,128)(2,1)S(1)}, bf16[512,768]{0,1:T(8,128)(2,1)}, u32[]{:S(2)}) copy-start(bf16[512,768]{0,1:T(8,128)(2,1)} %copy.53) | copy-start | bytes 2359300 | tf_op jit(solution)/shard_map/while
  923.0 19.1 %copy-start.9 = (bf16[512,3072]{1,0:T(8,128)(2,1)S(1)}, bf16[512,3072]{1,0:T(8,128)(2,1)}, u32[]{:S(2)}) copy-start(bf16[512,3072]{1,0:T(8,128)(2,1)} %copy-done.8) | copy-start | bytes 9437188 | tf_op jit(solution)/shard_map/while
  938.7 24.9 %collective-permute-start.2 = (bf16[1,512,768]{1,2,0:T(8,128)(2,1)}, bf16[1,512,768]{1,2,0:T(8,128)(2,1)}, u32[]{:S(2)}, u32[]{:S(2)}) collective-permute-start(bf16[1,512,768]{1,2,0:T(8,128)(2,1)} %slice.86), channel_id=1, source_target_pairs={{1,0},{3,2},{5,4},{7,6},{9,8},{11,10},{13,12},{15,14},{17,16},{19,... | collective-permute-start | bytes 2359304 | tf_op jit(solution)/shard_map/while/body/eval_jaxpr/ppermute | solution.py:17
  951.5 15.0 %collective-permute-start.3 = (bf16[1,512,768]{1,2,0:T(8,128)(2,1)S(1)}, bf16[1,512,768]{1,2,0:T(8,128)(2,1)S(1)}, u32[]{:S(2)}, u32[]{:S(2)}) collective-permute-start(bf16[1,512,768]{1,2,0:T(8,128)(2,1)S(1)} %slice.87), channel_id=1, source_target_pairs={{1,0},{3,2},{5,4},{7,6},{9,8},{11,10},{13,12},{15,14},{17,16},{19,... | collective-permute-start | bytes 2359304 | tf_op jit(solution)/shard_map/while/body/eval_jaxpr/ppermute | solution.py:17
  984.8 30.1 %reduce-scatter.7.cloned.1.call-start = ((), (), s32[]{:S(2)}) async-start(), calls=%async_computation.5 | async-start | bytes 1474560 | tf_op jit(solution)/shard_map/reduce_scatter | solution.py:234
  987.7 94.4 %reduce-scatter.5.cloned.1.call-start = ((), (), s32[]{:S(2)}) async-start(), calls=%async_computation.4 | async-start | bytes 4423680 | tf_op jit(solution)/shard_map/reduce_scatter | solution.py:234
  992.9 177.1 %reduce-scatter.9.cloned.1.call-start = ((), (), s32[]{:S(2)}) async-start(), calls=%async_computation.6 | async-start | bytes 5898240 | tf_op jit(solution)/shard_map/reduce_scatter | solution.py:234
  999.5 258.5 %reduce-scatter.11.cloned.1.call-start = ((), (), s32[]{:S(2)}) async-start(), calls=%async_computation.7 | async-start | bytes 5898240 | tf_op jit(solution)/shard_map/reduce_scatter | solution.py:234
  1006.0 252.1 %copy-start.49 = (u32[32]{0:T(128)S(1)}, u32[32]{0:T(128)}, u32[]{:S(2)}) copy-start(u32[32]{0:T(128)} %get-tuple-element.1116) | copy-start | bytes 388
  1006.0 254.0 %copy-start.39 = (f32[768]{0:T(1024)S(1)}, f32[768]{0:T(1024)}, u32[]{:S(2)}) copy-start(f32[768]{0:T(1024)} %get-tuple-element.421) | copy-start | bytes 9220
  1006.0 254.0 %copy-start.36 = (f32[768]{0:T(1024)S(1)}, f32[768]{0:T(1024)}, u32[]{:S(2)}) copy-start(f32[768]{0:T(1024)} %get-tuple-element.422) | copy-start | bytes 9220
  1006.0 254.0 %copy-start.33 = (f32[768]{0:T(1024)S(1)}, f32[768]{0:T(1024)}, u32[]{:S(2)}) copy-start(f32[768]{0:T(1024)} %get-tuple-element.424) | copy-start | bytes 9220
  1006.0 254.1 %copy-start.30 = (f32[768]{0:T(1024)S(1)}, f32[768]{0:T(1024)}, u32[]{:S(2)}) copy-start(f32[768]{0:T(1024)} %get-tuple-element.425) | copy-start | bytes 9220
  1006.0 254.1 %copy-start.27 = (f32[768]{0:T(1024)S(1)}, f32[768]{0:T(1024)}, u32[]{:S(2)}) copy-start(f32[768]{0:T(1024)} %get-tuple-element.426) | copy-start | bytes 9220
  1006.0 254.1 %copy-start.20 = (f32[3072]{0:T(1024)S(1)}, f32[3072]{0:T(1024)}, u32[]{:S(2)}) copy-start(f32[3072]{0:T(1024)} %get-tuple-element.430) | copy-start | bytes 36868
  1006.0 330.2 %all-reduce.33.cloned.1.call-start = ((), (), s32[]{:S(2)}) async-start(), calls=%async_computation.8 | async-start | bytes 7077888 | tf_op jit(solution)/shard_map/psum | solution.py:237
  (64 other events, 234.0 us)
Sparse Core Ops, SparseCore 0:
  10.9 72.4 all-gather.10
  85.0 28.5 all-gather.8
  115.2 89.1 all-gather.12
  205.9 87.8 all-gather.14
  496.2 68.3 all-gather.10
  565.9 28.7 all-gather.8
  596.3 89.1 all-gather.12
  687.1 87.8 all-gather.14
Sparse Core Ops, SparseCore 1:
  988.2 26.7 reduce-scatter.6
  1017.1 64.9 reduce-scatter.4
  1084.3 85.6 reduce-scatter.8
  1172.3 85.7 reduce-scatter.10
  1261.7 74.5 all-reduce.32
where the time goes:
time: 1360 us; the launch traced here: 1350 us
  waiting for transfers between devices  651 us (48%)
  matrix products  452 us (33%)
  blocking collectives  83.1 us (6%)
  other arithmetic  79.5 us (6%)
  local copies, waits for them, and re-layouts  45.5 us (3%)
  between operations  17.6 us (1%)
  starting transfers between devices  15.4 us (1%)
    reduce_scatter x4, waiting for transfers between devices, local(): lax.psum_scatter(for_sending(totals), 'fsdp', scatter_dimension=0, tiled=...  252 us
    all_gather x2, waiting for transfers between devices, micro(): lax.all_gather(shards[11], 'fsdp', axis=0, tiled=True)  165 us
    dot_general x2, matrix products, micro(): jnp.einsum('shqk,sqhd->skhd', d_scores, query_heads, preferred_element_ty...  108 us
    dot_general x2, matrix products, micro(): jnp.einsum('shqk,skhd->sqhd', d_scores, key_heads, preferred_element_type...  105 us
    all_gather x2, waiting for transfers between devices, micro(): lax.all_gather(shards[9], 'fsdp', axis=0, tiled=True)  102 us
    all_gather x2, waiting for transfers between devices, micro(): lax.all_gather(shards[0], 'fsdp', axis=0, tiled=True)  88.9 us
    dot_general x8, matrix products, outer_sum(): jnp.einsum('sri,srj->ij', left, right, preferred_element_type=jnp.float32)  56.7 us
    dot_general x8, matrix products, project(): jnp.einsum('sri,ij->srj', left, weight, preferred_element_type=jnp.float32)  46.1 us
  transfers between devices with their start and end apart: 21, of which 11 were waited for; matrix products, arithmetic and copies ran while one was open for 16% of the time, Pallas kernels for 0%

commit v1 on v0

v1 whole, which is shorter than its diff:
```python
from functools import partial

import jax
import jax.numpy as jnp
from jax import lax
from jax.experimental import pallas as pl
from jax.experimental.pallas import tpu as pltpu
from jax.sharding import PartitionSpec as P

H = 12
EPS = 1e-05
BF16 = jnp.bfloat16
F32 = jnp.float32
QB = 256


def norm_stats(values):
    center = values - jnp.mean(values, axis=-1, keepdims=True)
    inverse = lax.rsqrt(jnp.mean(center * center, axis=-1, keepdims=True) + EPS)
    return (center * inverse, inverse)


def norm_back(grad_norm, normal, inverse, gain):
    scaled = grad_norm * gain
    return inverse * (
        scaled
        - jnp.mean(scaled, axis=-1, keepdims=True)
        - normal * jnp.mean(scaled * normal, axis=-1, keepdims=True)
    )


def outer_sum(left, right):
    return jnp.einsum("sri,srj->ij", left, right, preferred_element_type=F32)


def project(left, weight):
    return jnp.einsum("sri,ij->srj", left, weight, preferred_element_type=F32)


def project_back(grad_rows, weight):
    return jnp.einsum("srj,ij->sri", grad_rows, weight, preferred_element_type=F32)


def dot_nt(a, b):
    return lax.dot_general(a, b, (((1,), (1,)), ((), ())), preferred_element_type=F32)


def dot_nn(a, b):
    return lax.dot_general(a, b, (((1,), (0,)), ((), ())), preferred_element_type=F32)


def head_mask(x, head, size):
    lane = lax.broadcasted_iota(jnp.int32, x.shape, 1)
    keep = (lane >= head * size) & (lane < (head + 1) * size)
    return jnp.where(keep, x, jnp.zeros_like(x))


def causal(scores_t, qb):
    n = scores_t.shape[0]
    bottom = scores_t[n - QB :]
    key = lax.broadcasted_iota(jnp.int32, bottom.shape, 0)
    query = lax.broadcasted_iota(jnp.int32, bottom.shape, 1)
    bottom = jnp.where(key <= query, bottom, -1e30)
    return bottom if n == QB else jnp.concatenate([scores_t[: n - QB], bottom], axis=0)


def attention_forward_kernel(factor, size, q_ref, k_ref, v_ref, o_ref, lse_ref):
    length = q_ref.shape[1]
    k = k_ref[0]
    vt = jnp.transpose(v_ref[0])
    for qb in range(length // QB):
        n = (qb + 1) * QB
        rows = pl.ds(qb * QB, QB)
        q = q_ref[0, rows, :]
        outs = []
        for head in range(2):
            s = causal(dot_nt(k[:n], head_mask(q, head, size)) * factor, qb)
            top = jnp.max(s, axis=0, keepdims=True)
            p = jnp.exp(s - top)
            total = jnp.sum(p, axis=0, keepdims=True)
            o = dot_nn(vt[head * size : (head + 1) * size, :n], p.astype(BF16))
            outs.append(o * (1.0 / total))
            lse_ref[0, 0, head : head + 1, rows] = top + jnp.log(total)
        o_ref[0, rows, :] = jnp.transpose(jnp.concatenate(outs, axis=0)).astype(o_ref.dtype)


def attention_forward(q, k, v, factor, size):
    mbs, length, width = q.shape
    lanes = 2 * size
    pairs = width // lanes
    block = pl.BlockSpec((1, length, lanes), lambda m, p: (m, 0, p))
    area = mbs * pairs * 2 * length * (length + QB) // 2
    return pl.pallas_call(
        partial(attention_forward_kernel, factor, size),
        grid=(mbs, pairs),
        in_specs=[block] * 3,
        out_specs=[block, pl.BlockSpec((1, 1, 8, length), lambda m, p: (m, p, 0, 0))],
        out_shape=[
            jax.ShapeDtypeStruct(q.shape, BF16),
            jax.ShapeDtypeStruct((mbs, pairs, 8, length), F32),
        ],
        compiler_params=pltpu.CompilerParams(vmem_limit_bytes=48 << 20),
        cost_estimate=pl.CostEstimate(
            flops=16 * area * size, bytes_accessed=8 * q.size, transcendentals=area
        ),
        name="attention_forward",
    )(q, k, v)


def attention_backward_kernel(factor, size, q_ref, k_ref, v_ref, do_ref, lse_ref, dq_ref, dk_ref, dv_ref, dk_sum, dv_sum):
    length = q_ref.shape[1]
    k = k_ref[0]
    v = v_ref[0]
    kt = jnp.transpose(k)
    for qb in reversed(range(length // QB)):
        n = (qb + 1) * QB
        rows = pl.ds(qb * QB, QB)
        q = q_ref[0, rows, :]
        do = do_ref[0, rows, :]
        dqs, dk, dv = [], None, None
        for head in range(2):
            qh = head_mask(q, head, size)
            doh = head_mask(do, head, size)
            s = causal(dot_nt(k[:n], qh) * factor, qb)
            p = jnp.exp(s - lse_ref[0, 0, head : head + 1, rows])
            dp = dot_nt(v[:n], doh)
            mean = jnp.sum(dp * p, axis=0, keepdims=True)
            ds = (p * (dp - mean) * factor).astype(BF16)
            dvh = dot_nn(p.astype(BF16), doh)
            dkh = dot_nn(ds, qh)
            dv = dvh if dv is None else dv + dvh
            dk = dkh if dk is None else dk + dkh
            dqs.append(dot_nn(kt[head * size : (head + 1) * size, :n], ds))
        dq_ref[0, rows, :] = jnp.transpose(jnp.concatenate(dqs, axis=0)).astype(BF16)
        if n == length:
            dk_sum[...] = dk
            dv_sum[...] = dv
        else:
            dk_sum[:n] += dk
            dv_sum[:n] += dv
    dk_ref[0] = dk_sum[...].astype(BF16)
    dv_ref[0] = dv_sum[...].astype(BF16)


def attention_backward(q, k, v, do, lse, factor, size):
    mbs, length, width = q.shape
    lanes = 2 * size
    pairs = width // lanes
    block = pl.BlockSpec((1, length, lanes), lambda m, p: (m, 0, p))
    area = mbs * pairs * 2 * length * (length + QB) // 2
    return pl.pallas_call(
        partial(attention_backward_kernel, factor, size),
        grid=(mbs, pairs),
        in_specs=[block] * 4 + [pl.BlockSpec((1, 1, 8, length), lambda m, p: (m, p, 0, 0))],
        out_specs=[block] * 3,
        out_shape=[jax.ShapeDtypeStruct(q.shape, BF16)] * 3,
        scratch_shapes=[pltpu.VMEM((length, lanes), F32)] * 2,
        compiler_params=pltpu.CompilerParams(vmem_limit_bytes=48 << 20),
        cost_estimate=pl.CostEstimate(
            flops=40 * area * size, bytes_accessed=14 * q.size, transcendentals=area
        ),
        name="attention_backward",
    )(q, k, v, do, lse)


def local(
    inputs,
    weight_qkv,
    bias_query,
    bias_value,
    weight_mix,
    bias_mix,
    gain_attn,
    shift_attn,
    gain_mlp,
    shift_mlp,
    weight_up,
    bias_up,
    weight_down,
    bias_down,
    cotangent,
):
    width = weight_qkv.shape[1] // 3
    half = width // 2
    size = width // H
    factor = size ** (-0.5)
    rows = inputs.shape[2]
    owners = lax.axis_size("fsdp")
    reps = lax.axis_size("rep")
    ctx = lax.axis_index("ctx")
    rep = lax.axis_index("rep")
    own = weight_qkv.shape[0]

    def swap(x):
        return lax.ppermute(x, "ctx", [(0, 1), (1, 0)])

    def order(mine, other, axis):
        return jnp.where(
            ctx == 0,
            jnp.concatenate([mine, other], axis=axis),
            jnp.concatenate([other, mine], axis=axis),
        )

    def columns(x, axis, which):
        return lax.dynamic_slice_in_dim(x, which * half, half, axis)

    flat = jnp.concatenate(
        [bias_query, bias_value, bias_mix, gain_attn, shift_attn, gain_mlp, shift_mlp, bias_down, bias_up]
    )
    small = lax.all_gather(flat.reshape(1, -1), "fsdp", axis=0, tiled=True).astype(F32)
    b_query, b_value, b_mix, g_attn, s_attn, g_mlp, s_mlp, b_down = (
        small[:, i * own : (i + 1) * own].reshape(-1) for i in range(8)
    )
    b_up = small[:, 8 * own :].reshape(-1)

    part = own // reps
    mine = lax.dynamic_slice_in_dim(weight_qkv, rep * part, part, 0)
    mine = jnp.concatenate([columns(mine[:, i * width : (i + 1) * width], 1, ctx) for i in range(3)], axis=1)
    w_qkv = lax.all_gather(mine, ("fsdp", "rep"), axis=0, tiled=True)

    def gather(shard):
        piece = shard.shape[0] // (2 * reps)
        mine = lax.dynamic_slice_in_dim(shard, (rep * 2 + ctx) * piece, piece, 0)
        return lax.all_gather(mine, ("fsdp", "rep", "ctx"), axis=0, tiled=True)

    w_mix = gather(weight_mix)
    w_up = gather(weight_up)
    w_down = gather(weight_down)

    tokens = inputs[:, 0].astype(F32)
    normal_one, inverse_one = norm_stats(tokens)
    first_own = (normal_one * g_attn + s_attn).astype(BF16)
    first = order(first_own, swap(first_own), 1)
    joined = project(first, w_qkv)
    query = (joined[..., :half] + columns(b_query, 0, ctx)).astype(BF16)
    key = joined[..., half : 2 * half].astype(BF16)
    value = (joined[..., 2 * half :] + columns(b_value, 0, ctx)).astype(BF16)
    mixed_heads, lse = attention_forward(query, key, value, factor, size)

    def my_rows(x):
        return lax.dynamic_slice_in_dim(x, ctx * rows, rows, 1)

    def their_rows(x):
        return lax.dynamic_slice_in_dim(x, (1 - ctx) * rows, rows, 1)

    mixed = order(my_rows(mixed_heads), swap(their_rows(mixed_heads)), 2)
    middle = tokens + project(mixed, w_mix) + b_mix
    normal_two, inverse_two = norm_stats(middle)
    second = (normal_two * g_mlp + s_mlp).astype(BF16)
    before = project(second, w_up) + b_up
    active, gelu_back = jax.vjp(partial(jax.nn.gelu, approximate=True), before)
    active = active.astype(BF16)
    result = (middle + project(active, w_down) + b_down).astype(BF16)

    d_down = cotangent[:, 0]
    grad_out = d_down.astype(F32)
    g_wdown = outer_sum(active, d_down)
    g_bdown = jnp.sum(grad_out, axis=(0, 1))
    d_before_f = gelu_back(project_back(d_down, w_down))[0]
    d_before = d_before_f.astype(BF16)
    g_wup = outer_sum(second, d_before)
    g_bup = jnp.sum(d_before.astype(F32), axis=(0, 1))
    d_second = project_back(d_before, w_up)
    g_gmlp = jnp.sum(d_second * normal_two, axis=(0, 1))
    g_smlp = jnp.sum(d_second, axis=(0, 1))
    d_middle = grad_out + norm_back(d_second, normal_two, inverse_two, g_mlp)
    d_branch = d_middle.astype(BF16)
    g_wmix = outer_sum(mixed, d_branch)
    g_bmix = jnp.sum(d_branch.astype(F32), axis=(0, 1))
    d_mixed = project_back(d_branch, w_mix).astype(BF16)
    d_heads = order(columns(d_mixed, 2, ctx), swap(columns(d_mixed, 2, 1 - ctx)), 1)
    d_query, d_key, d_value = attention_backward(query, key, value, d_heads, lse, factor, size)
    d_joined = jnp.concatenate([d_query, d_key, d_value], axis=-1)
    g_wqkv = outer_sum(first, d_joined)
    g_bquery = jnp.sum(d_query.astype(F32), axis=(0, 1))
    g_bvalue = jnp.sum(d_value.astype(F32), axis=(0, 1))
    d_first = project_back(d_joined, w_qkv)
    d_first = my_rows(d_first) + swap(their_rows(d_first).astype(BF16)).astype(F32)
    g_gattn = jnp.sum(d_first * normal_one, axis=(0, 1))
    g_sattn = jnp.sum(d_first, axis=(0, 1))
    d_tokens = d_middle + norm_back(d_first, normal_one, inverse_one, g_attn)

    def reduce(grad):
        piece = lax.psum_scatter(
            grad.astype(BF16), ("fsdp", "rep", "ctx"), scatter_dimension=0, tiled=True
        )
        return lax.all_gather(piece, ("rep", "ctx"), axis=0, tiled=True).astype(F32)

    o_wdown = reduce(g_wdown)
    o_wup = reduce(g_wup)
    o_wmix = reduce(g_wmix)
    piece = lax.psum_scatter(g_wqkv.astype(BF16), ("fsdp", "rep"), scatter_dimension=0, tiled=True)
    piece = lax.all_gather(piece, "rep", axis=0, tiled=True)
    other = swap(piece)
    low, high = jnp.where(ctx == 0, piece, other), jnp.where(ctx == 0, other, piece)
    o_wqkv = jnp.concatenate(
        [t for i in range(3) for t in (low[:, i * half : (i + 1) * half], high[:, i * half : (i + 1) * half])],
        axis=1,
    ).astype(F32)

    zeros = jnp.zeros((width,), F32)

    def place(v):
        return lax.dynamic_update_slice_in_dim(zeros, v, ctx * half, 0)

    vectors = (place(g_bquery), place(g_bvalue), g_bmix, g_gattn, g_sattn, g_gmlp, g_smlp, g_bdown)
    stacked = jnp.concatenate([v.reshape(owners, own) for v in vectors] + [g_bup.reshape(owners, -1)], axis=1)
    summed = lax.psum(stacked, ("rep", "fsdp", "ctx"))
    summed = lax.dynamic_slice_in_dim(summed, lax.axis_index("fsdp"), 1, 0)[0]
    o_bq, o_bv, o_bmix, o_ga, o_sa, o_gm, o_sm, o_bd = (summed[i * own : (i + 1) * own] for i in range(8))
    o_bup = summed[8 * own :]
    return (
        result[:, None],
        d_tokens[:, None],
        o_wqkv,
        o_bq,
        o_bv,
        o_wmix,
        o_bmix,
        o_ga,
        o_sa,
        o_gm,
        o_sm,
        o_wup,
        o_bup,
        o_wdown,
        o_bd,
    )


def solution(mesh):
    row = P(None, ("rep", "fsdp"), "ctx", None)
    mat = P("fsdp", None)
    vec = P("fsdp")
    params = (mat, vec, vec, mat, vec, vec, vec, vec, vec, mat, vec, mat, vec)
    in_specs = (row,) + params + (row,)
    out_specs = (row, row) + params
    return jax.shard_map(local, mesh=mesh, in_specs=in_specs, out_specs=out_specs, check_vma=False)
```

time: 1360 us -> 809 us (0.59)
  matrix products: 452 us -> 108 us
  waiting for transfers between devices: 651 us -> 478 us
  Pallas kernels: 0 us -> 57.3 us
  other arithmetic: 79.5 us -> 31.1 us
  local copies, waits for them, and re-layouts: 45.5 us -> 26.5 us
    dot_general x36 -> x12, matrix products: 452 us -> 108 us  [the longest x4 36.6 us: project(): return jnp.einsum('sri,ij->srj', left, weight, preferred_element_type=F32)]
    all_gather x8 -> x6, waiting for transfers between devices: 356 us -> 163 us  [the longest x3 133 us: gather(): return lax.all_gather(mine, ('fsdp', 'rep', 'ctx'), axis=0, tiled=True)]
    reduce_scatter x4, waiting for transfers between devices: 252 us -> 311 us  [the longest x3 198 us: reduce(): lax.psum_scatter(grad.astype(BF16), ('fsdp', 'rep', 'ctx'), scatter_dimen...]
    pallas_call x0 -> x2, Pallas kernels: none -> 57.3 us  [the longest x1 31.8 us: attention_backward(): pl.pallas_call(partial(attention_backward_kernel, factor, size), grid=(mb...]
    psum x1 -> x0, waiting for transfers between devices: 39.6 us -> none  [local(): lax.psum(for_sending(shares), ('rep', 'ctx'))]
    while x2 -> x0, blocking collectives: 31.6 us -> none
    psum x1, blocking collectives: 16.1 us -> 41.2 us  [local(): summed = lax.psum(stacked, ('rep', 'fsdp', 'ctx'))]
    convert_element_type x48 -> x6, other arithmetic: 35 us -> 11.4 us  [the longest x3 6.64 us: reduce(): return lax.all_gather(piece, ('rep', 'ctx'), axis=0, tiled=True).astype(F32)]
  transfers between devices with their start and end apart: 21 -> 15, of which waited for: 11 -> 10; matrix products, arithmetic and copies ran while one was open for 16% -> 16% of each run, Pallas kernels for 0% -> 7%
where the time goes in v1:
time: 809 us; the launch traced here: 800 us
  waiting for transfers between devices  478 us (59%)
  matrix products  108 us (13%)
  blocking collectives  73.2 us (9%)
  Pallas kernels  57.3 us (7%)
  other arithmetic  31.1 us (4%)
  local copies, waits for them, and re-layouts  26.5 us (3%)
  between operations  15.1 us (2%)
  starting transfers between devices  10.8 us (1%)
    reduce_scatter x3, waiting for transfers between devices, reduce(): lax.psum_scatter(grad.astype(BF16), ('fsdp', 'rep', 'ctx'), scatter_dimen...  198 us
    all_gather x3, waiting for transfers between devices, gather(): return lax.all_gather(mine, ('fsdp', 'rep', 'ctx'), axis=0, tiled=True)  133 us
    reduce_scatter x1, waiting for transfers between devices, local(): lax.psum_scatter(g_wqkv.astype(BF16), ('fsdp', 'rep'), scatter_dimension=...  114 us
    psum x1, blocking collectives, local(): summed = lax.psum(stacked, ('rep', 'fsdp', 'ctx'))  41.2 us
    dot_general x4, matrix products, project(): return jnp.einsum('sri,ij->srj', left, weight, preferred_element_type=F32)  36.6 us
    dot_general x4, matrix products, project_back(): jnp.einsum('srj,ij->sri', grad_rows, weight, preferred_element_type=F32)  36.3 us
    dot_general x4, matrix products, outer_sum(): return jnp.einsum('sri,srj->ij', left, right, preferred_element_type=F32)  34.9 us
    pallas_call x1, Pallas kernels, attention_backward(): pl.pallas_call(partial(attention_backward_kernel, factor, size), grid=(mb...  31.8 us
  transfers between devices with their start and end apart: 15, of which 10 were waited for; matrix products, arithmetic and copies ran while one was open for 16% of the time, Pallas kernels for 7%

profile of v1, /device:TPU:1, one launch (start us, length us, event | category | flops | bytes accessed | tf_op | source)
XLA Modules:
  0.0 799.7 jit_solution(8555902424170331080)
XLA Ops:
  9.0 1.4 constant_dynamic-slice_fusion.5
  11.2 1.6 constant_dynamic-slice_fusion.3
  12.9 6.1 concatenate.33
  19.0 11.6 %all-gather.1 = bf16[4,1,2304]{2,1,0:T(2,128)(2,1)S(1)} all-gather(bf16[1,1,2304]{2,1,0:T(2,128)(2,1)S(1)} %reshape.139), channel_id=2, replica_groups=mesh['rep'=4,'fsdp'=4,'ctx'=2] {'fsdp'}, dimensions={0}, use_global_device_ids=true | all-gather | bytes 23040 | tf_op jit(solution)/shard_map/all_gather | solution.py:210
  31.5 1.7 convert_reduce_fusion.2
  33.8 1.8 fusion.30
  35.6 3.3 collective-permute-start
  39.2 3.1 collective-permute-done
  42.2 29.1 %all-gather.9.cloned.1.call-done = bf16[768,1152]{1,0:T(8,128)(2,1)} async-done(((bf16[48,1152]{1,0:T(8,128)(2,1)}), bf16[768,1152]{1,0:T(8,128)(2,1)}) %all-gather.9.cloned.1.call-update) | async-done | bytes 1769488 | tf_op jit(solution)/shard_map/all_gather | solution.py:219
  71.4 7.3 fusion.43
  78.9 1.7 fusion.39
  80.6 25.5 %attention_forward.1 = (bf16[2,1024,384]{2,1,0:T(8,128)(2,1)S(1)}, f32[2,3,8,1024]{3,2,1,0:T(8,128)S(1)}) custom-call(bf16[2,1024,384]{2,1,0:T(8,128)(2,1)S(1)} %get-tuple-element.67.q_ref, bf16[2,1024,384]{2,1,0:T(8,128)(2,1)S(1)} %slice.188.k_ref, bf16[2,1024,384]{2,1,0:T(8,128)(2,1)} %get-tuple-element.66.v_ref), custom_call_target="tpu_custom_call" | custom-call | flops 8053063680 | bytes 6291456 | tf_op jit(solution)/shard_map/attention_forward/pallas_call | solution.py:93
  107.2 1.9 collective-permute-start.1
  109.4 19.6 %all-gather.11.cloned.1.call-done = bf16[768,768]{1,0:T(8,128)(2,1)} async-done(((bf16[24,768]{1,0:T(8,128)(2,1)}), bf16[768,768]{1,0:T(8,128)(2,1)}) %all-gather.11.cloned.1.call-update) | async-done | bytes 1179664 | tf_op jit(solution)/shard_map/all_gather | solution.py:224
  128.9 4.8 fusion.63
  133.8 2.4 multiply_reduce_fusion.2
  136.2 58.3 %all-gather.13.cloned.1.call-done = bf16[768,3072]{1,0:T(8,128)(2,1)} async-done(((bf16[24,3072]{1,0:T(8,128)(2,1)}), bf16[768,3072]{1,0:T(8,128)(2,1)}) %all-gather.13.cloned.1.call-update) | async-done | bytes 4718608 | tf_op jit(solution)/shard_map/all_gather | solution.py:224
  194.4 10.9 %fusion.16 = f32[2,512,3072]{2,1,0:T(8,128)} fusion(bf16[768,3072]{1,0:T(8,128)(2,1)} %all-gather.13.cloned.1.call-done, f32[2,512,768]{2,1,0:T(8,128)} %get-tuple-element.95, f32[768]{0:T(1024)S(1)} %add.172, f32[768]{0:T(1024)S(1)} %mul.189, f32[2,512]{1,0:T(2,128)S(1)} %add_rsqrt_fusion, f32[2,512]{1,0:T(2,128)S(1)} %broadcast_multiply_fusion.4), kind=kOutput, calls=%fused_computation.24 | convolution fusion | flops 4835770368 | bytes 20461568 | tf_op jit(solution)/shard_map/sri,ij->srj/dot_general | solution.py:37
  205.3 54.9 %all-gather.15.cloned.1.call-done = bf16[3072,768]{1,0:T(8,128)(2,1)} async-done(((bf16[96,768]{1,0:T(8,128)(2,1)}), bf16[3072,768]{1,0:T(8,128)(2,1)}) %all-gather.15.cloned.1.call-update) | async-done | bytes 4718608 | tf_op jit(solution)/shard_map/all_gather | solution.py:224
  260.2 15.2 %convert_reduce_fusion = (f32[3072]{0:T(1024)S(1)}, bf16[2,512,3072]{2,1,0:T(8,128)(2,1)S(1)}) fusion(f32[2,512,3072]{2,1,0:T(8,128)} %fusion.16, f32[3072]{0:T(1024)S(1)} %add.175, bf16[2,1,512,768]{3,2,1,0:T(8,128)(2,1)S(1)} %copy-done.7, bf16[3072,768]{1,0:T(8,128)(2,1)} %all-gather.15.cloned.1.call-done), kind=kOutput, calls=%fused_computation.14 | convolution fusion | flops 4904186880 | bytes 25190400 | tf_op jit(solution)/shard_map/srj,ij->sri/dot_general | solution.py:41
  275.4 2.6 copy-done.19
  278.1 9.7 %bitcast_convert_fusion.1 = bf16[768,3072]{1,0:T(8,128)(2,1)} fusion(bf16[2,512,3072]{2,1,0:T(8,128)(2,1)S(1)} %get-tuple-element.98, f32[2,512,768]{2,1,0:T(8,128)} %get-tuple-element.95, f32[768]{0:T(1024)S(1)} %add.172, f32[768]{0:T(1024)S(1)} %mul.189, f32[2,512]{1,0:T(2,128)S(1)} %add_rsqrt_fusion, f32[2,512]{1,0:T(2,128)S(1)} %broadcast_multiply_fusion.4), kind=kOutput, calls=%fused_computation.17 | convolution fusion | flops 4838129664 | bytes 14170112 | tf_op jit(solution)/shard_map/sri,srj->ij/dot_general | solution.py:33
  287.9 9.8 %multiply_reduce_fusion = (f32[768]{0:T(1024)S(1)}, f32[2,512]{1,0:T(2,128)S(1)}, f32[2,512]{1,0:T(2,128)S(1)}, f32[768]{0:T(1024)S(1)}, f32[2,512,768]{2,1,0:T(8,128)S(1)}) fusion(f32[2,512,768]{2,1,0:T(8,128)} %get-tuple-element.95, f32[2,512]{1,0:T(2,128)S(1)} %add_rsqrt_fusion, f32[2,512]{1,0:T(2,128)S(1)} %broadcast_multiply_fusion.4, ...), kind=kOutput, calls=%fused_computation.56 | convolution fusion | flops 4838912000 | bytes 17327104 | tf_op jit(solution)/shard_map/srj,ij->sri/dot_general | solution.py:41
  297.7 3.0 convert_reduce_fusion.3
  300.7 1.4 convolution_convert_fusion
  303.3 3.9 bitcast_convert_fusion.2
  307.5 1.6 maximum_select_fusion.2.do_ref
  309.1 31.8 %attention_backward.1 = (bf16[2,1024,384]{2,1,0:T(8,128)(2,1)S(1)}, bf16[2,1024,384]{2,1,0:T(8,128)(2,1)S(1)}, bf16[2,1024,384]{2,1,0:T(8,128)(2,1)S(1)}) custom-call(bf16[2,1024,384]{2,1,0:T(8,128)(2,1)} %copy-done.3, bf16[2,1024,384]{2,1,0:T(8,128)(2,1)} %copy-done.2, bf16[2,1024,384]{2,1,0:T(8,128)(2,1)} %get-tuple-element.66.v_ref, ...), custom_call_target="tpu_custom_call" | custom-call | flops 20132659200 | bytes 11010048 | tf_op jit(solution)/shard_map/attention_backward/pallas_call | solution.py:151
  341.7 2.2 copy-done.10
  343.9 8.7 %fusion.28 = bf16[768,1152]{1,0:T(8,128)(2,1)} fusion(bf16[2,1024,1152]{2,1,0:T(8,128)(2,1)S(1)} %constant_dynamic-update-slice_fusion, bf16[2,512,768]{2,1,0:T(8,128)(2,1)} %collective-permute-done, bf16[2,512,768]{2,1,0:T(8,128)(2,1)} %fusion.30, pred[]{:T(512)S(6)} %eq.2), kind=kOutput, calls=%fused_computation.39 | convolution fusion | flops 3638919168 | bytes 9633793 | tf_op jit(solution)/shard_map/sri,srj->ij/dot_general | solution.py:33
  352.9 12.6 %bitcast_convert_fusion = bf16[3072,768]{1,0:T(8,128)(2,1)} fusion(bf16[2,1,512,768]{3,2,1,0:T(8,128)(2,1)} %param.29, f32[2,512,3072]{2,1,0:T(8,128)} %fusion.16, f32[3072]{0:T(1024)S(1)} %add.175), kind=kOutput, calls=%fused_computation.16 | convolution fusion | flops 4865654784 | bytes 18886656 | tf_op jit(solution)/shard_map/sri,srj->ij/dot_general | solution.py:33
  366.2 9.9 %fusion.41 = f32[2,1024,768]{2,1,0:T(8,128)} fusion(bf16[2,1024,1152]{2,1,0:T(8,128)(2,1)} %copy-done.10, bf16[768,1152]{1,0:T(8,128)(2,1)} %all-gather.9.cloned.1.call-done), kind=kOutput, calls=%fused_computation.70 | convolution fusion | flops 3623878656 | bytes 12779520 | tf_op jit(solution)/shard_map/srj,ij->sri/dot_general | solution.py:41
  376.1 3.2 dynamic-slice_convert_fusion
  379.5 12.3 %reduce-scatter.9.cloned.1.call-done = bf16[24,3072]{1,0:T(8,128)(2,1)} async-done(((bf16[768,3072]{1,0:T(8,128)(2,1)}), bf16[24,3072]{1,0:T(8,128)(2,1)}) %reduce-scatter.9.cloned.1.call-update) | async-done | bytes 147472 | tf_op jit(solution)/shard_map/reduce_scatter | solution.py:284
  392.2 13.4 %fusion.49 = bf16[2,1,512,768]{3,2,1,0:T(8,128)(2,1)} fusion(f32[768]{0:T(1024)S(1)} %add.182, f32[2,512,768]{2,1,0:T(8,128)} %get-tuple-element.95, bf16[3072,768]{1,0:T(8,128)(2,1)} %all-gather.15.cloned.1.call-done, f32[2,512,3072]{2,1,0:T(8,128)} %fusion.16, f32[3072]{0:T(1024)S(1)} %add.175), kind=kOutput, calls=%fused_computation.79 | convolution fusion | flops 4865654784 | bytes 22035456 | tf_op jit(solution)/shard_map/sri,ij->srj/dot_general | solution.py:37
  407.2 85.8 %reduce-scatter.7.cloned.1.call-done = bf16[24,768]{1,0:T(8,128)(2,1)} async-done(((bf16[768,768]{1,0:T(8,128)(2,1)}), bf16[24,768]{1,0:T(8,128)(2,1)}) %reduce-scatter.7.cloned.1.call-update) | async-done | bytes 36880 | tf_op jit(solution)/shard_map/reduce_scatter | solution.py:284
  493.0 11.6 %all_gather.33 = bf16[192,768]{1,0:T(8,128)(2,1)S(1)} all-gather(bf16[24,768]{1,0:T(8,128)(2,1)} %reduce-scatter.7.cloned.1.call-done), channel_id=1, replica_groups=mesh['rep'=4,'fsdp'=4,'ctx'=2] {'rep','ctx'}, dimensions={0}, use_global_device_ids=true | all-gather | bytes 331776 | tf_op jit(solution)/shard_map/all_gather | solution.py:287
  505.5 4.5 fusion.36
  510.0 113.8 %reduce-scatter.5.cloned.1.call-done = bf16[48,1152]{1,0:T(8,128)(2,1)} async-done(((bf16[768,1152]{1,0:T(8,128)(2,1)}), bf16[48,1152]{1,0:T(8,128)(2,1)}) %reduce-scatter.5.cloned.1.call-update) | async-done | bytes 110608 | tf_op jit(solution)/shard_map/reduce_scatter | solution.py:292
  623.8 8.7 %all_gather.32 = bf16[192,1152]{1,0:T(8,128)(2,1)S(1)} all-gather(bf16[48,1152]{1,0:T(8,128)(2,1)} %reduce-scatter.5.cloned.1.call-done), channel_id=1, replica_groups=mesh['rep'=4,'fsdp'=4,'ctx'=2] {'rep'}, dimensions={0}, use_global_device_ids=true | all-gather | bytes 552960 | tf_op jit(solution)/shard_map/all_gather | solution.py:293
  632.6 4.0 collective-permute-start.4
  636.6 99.6 %reduce-scatter.11.cloned.1.call-done = bf16[96,768]{1,0:T(8,128)(2,1)} async-done(((bf16[3072,768]{1,0:T(8,128)(2,1)}), bf16[96,768]{1,0:T(8,128)(2,1)}) %reduce-scatter.11.cloned.1.call-update) | async-done | bytes 147472 | tf_op jit(solution)/shard_map/reduce_scatter | solution.py:284
  736.2 4.5 fusion.35
  741.0 41.2 %psum.7 = f32[4,2304]{1,0:T(4,128)S(1)} all-reduce(f32[4,2304]{1,0:T(4,128)S(1)} %concatenate.43), channel_id=1, replica_groups=mesh['rep'=4,'fsdp'=4,'ctx'=2] {'rep','fsdp','ctx'}, use_global_device_ids=true, to_apply=%region_18.19 | all-reduce | flops 9216 | bytes 73728 | tf_op jit(solution)/shard_map/psum | solution.py:308
  783.9 1.3 convert_element_type.98
  785.2 2.9 convert_element_type.106
  788.1 1.4 all-gather.19.cloned.1.call-done
  789.5 2.8 convert_element_type.108
  (123 shorter events, 14.0 us)
Async XLA Ops:
  7.2 3.3 copy-start
  7.2 26.0 %copy-start.4 = (bf16[2,1,512,768]{3,2,1,0:T(8,128)(2,1)S(1)}, bf16[2,1,512,768]{3,2,1,0:T(8,128)(2,1)}, u32[]{:S(2)}) copy-start(bf16[2,1,512,768]{3,2,1,0:T(8,128)(2,1)} %param.15) | copy-start | bytes 4718596
  7.2 64.2 %all-gather.9.cloned.1.call-start = ((), (), s32[]{:S(2)}) async-start(), calls=%async_computation.4 | async-start | bytes 1880064 | tf_op jit(solution)/shard_map/all_gather | solution.py:219
  8.9 120.0 %all-gather.11.cloned.1.call-start = ((), (), s32[]{:S(2)}) async-start(), calls=%async_computation.5 | async-start | bytes 1216512 | tf_op jit(solution)/shard_map/all_gather | solution.py:224
  10.4 184.0 %all-gather.13.cloned.1.call-start = ((), (), s32[]{:S(2)}) async-start(), calls=%async_computation.6 | async-start | bytes 4866048 | tf_op jit(solution)/shard_map/all_gather | solution.py:224
  11.2 249.1 %all-gather.15.cloned.1.call-start = ((), (), s32[]{:S(2)}) async-start(), calls=%async_computation.7 | async-start | bytes 4866048 | tf_op jit(solution)/shard_map/all_gather | solution.py:224
  12.8 379.0 %reduce-scatter.9.cloned.1.call-start = ((), (), s32[]{:S(2)}) async-start(), calls=%async_computation.10 | async-start | bytes 4866048 | tf_op jit(solution)/shard_map/reduce_scatter | solution.py:284
  31.4 4.2 copy-start.13
  33.2 45.6 %copy-start.11 = (f32[2,512]{1,0:T(2,128)}, f32[2,512]{1,0:T(2,128)S(1)}, u32[]{:S(2)}) copy-start(f32[2,512]{1,0:T(2,128)S(1)} %broadcast_multiply_fusion.5) | copy-start | bytes 12292
  33.8 44.9 %copy-start.15 = (f32[2,512]{1,0:T(2,128)}, f32[2,512]{1,0:T(2,128)S(1)}, u32[]{:S(2)}) copy-start(f32[2,512]{1,0:T(2,128)S(1)} %add_rsqrt_fusion.1) | copy-start | bytes 12292
  35.6 6.6 collective-permute-start
  78.9 1.7 copy-start.2
  80.6 25.5 %copy-start.3 = (bf16[2,1024,384]{2,1,0:T(8,128)(2,1)}, bf16[2,1024,384]{2,1,0:T(8,128)(2,1)S(1)}, u32[]{:S(2)}) copy-start(bf16[2,1024,384]{2,1,0:T(8,128)(2,1)S(1)} %get-tuple-element.67.q_ref) | copy-start | bytes 4718596
  107.2 26.6 %copy-start.8 = (bf16[2,512,384]{2,1,0:T(8,128)(2,1)}, bf16[2,512,384]{2,1,0:T(8,128)(2,1)S(1)}, u32[]{:S(2)}) copy-start(bf16[2,512,384]{2,1,0:T(8,128)(2,1)S(1)} %get-tuple-element.71) | copy-start | bytes 2359300
  107.2 21.7 %collective-permute-start.1 = (bf16[2,512,384]{2,1,0:T(8,128)(2,1)}, bf16[2,512,384]{2,1,0:T(8,128)(2,1)}, u32[]{:S(2)}, u32[]{:S(2)}) collective-permute-start(bf16[2,512,384]{2,1,0:T(8,128)(2,1)} %get-tuple-element.72), channel_id=1, source_target_pairs={{0,1},{1,0},{2,3},{3,2},{4,5},{5,4},{6,7},{7,6},{8,9},{9,8},{10,11... | collective-permute-start | bytes 2359304 | tf_op jit(solution)/shard_map/ppermute | solution.py:195
  136.1 124.1 %copy-start.7 = (bf16[2,1,512,768]{3,2,1,0:T(8,128)(2,1)S(1)}, bf16[2,1,512,768]{3,2,1,0:T(8,128)(2,1)}, u32[]{:S(2)}) copy-start(bf16[2,1,512,768]{3,2,1,0:T(8,128)(2,1)} %param.29) | copy-start | bytes 4718596
  275.4 2.6 copy-start.19
  287.8 205.2 %reduce-scatter.7.cloned.1.call-start = ((), (), s32[]{:S(2)}) async-start(), calls=%async_computation.9 | async-start | bytes 1216512 | tf_op jit(solution)/shard_map/reduce_scatter | solution.py:284
  297.7 3.0 copy-start.18
  300.7 2.0 copy-start.6
  302.2 1.1 copy-start.9
  302.4 5.1 collective-permute-start.2
  307.3 316.5 %reduce-scatter.5.cloned.1.call-start = ((), (), s32[]{:S(2)}) async-start(), calls=%async_computation.8 | async-start | bytes 1880064 | tf_op jit(solution)/shard_map/reduce_scatter | solution.py:292
  341.7 2.2 copy-start.10
  352.6 383.6 %reduce-scatter.11.cloned.1.call-start = ((), (), s32[]{:S(2)}) async-start(), calls=%async_computation.12 | async-start | bytes 4866048 | tf_op jit(solution)/shard_map/reduce_scatter | solution.py:284
  365.5 0.7 copy-start.17
  365.5 419.7 %all-gather.17.cloned.1.call-start = ((), (), s32[]{:S(2)}) async-start(), calls=%async_computation.11 | async-start | bytes 1327104 | tf_op jit(solution)/shard_map/all_gather | solution.py:287
  379.3 126.2 %collective-permute-start.3 = (bf16[2,512,768]{2,1,0:T(8,128)(2,1)}, bf16[2,512,768]{2,1,0:T(8,128)(2,1)}, u32[]{:S(2)}, u32[]{:S(2)}) collective-permute-start(bf16[2,512,768]{2,1,0:T(8,128)(2,1)} %dynamic-slice_convert_fusion), channel_id=1, source_target_pairs={{0,1},{1,0},{2,3},{3,2},{4,5},{5,4},{6,7},{7,6},{8,9},{9,8},{10,11... | collective-permute-start | bytes 4718600 | tf_op jit(solution)/shard_map/ppermute | solution.py:195
  391.9 397.7 %all-gather.19.cloned.1.call-start = ((), (), s32[]{:S(2)}) async-start(), calls=%async_computation.13 | async-start | bytes 1327104 | tf_op jit(solution)/shard_map/all_gather | solution.py:287
  405.6 99.8 %copy-start.12 = (f32[2,512]{1,0:T(2,128)S(1)}, f32[2,512]{1,0:T(2,128)}, u32[]{:S(2)}) copy-start(f32[2,512]{1,0:T(2,128)} %copy-done.11) | copy-start | bytes 12292
  405.6 99.8 %copy-start.14 = (f32[768]{0:T(1024)S(1)}, f32[768]{0:T(1024)}, u32[]{:S(2)}) copy-start(f32[768]{0:T(1024)} %copy-done.13) | copy-start | bytes 9220
  405.6 99.8 %copy-start.16 = (f32[2,512]{1,0:T(2,128)S(1)}, f32[2,512]{1,0:T(2,128)}, u32[]{:S(2)}) copy-start(f32[2,512]{1,0:T(2,128)} %copy-done.15) | copy-start | bytes 12292
  406.3 99.2 %copy-start.5 = (bf16[2,1,512,768]{3,2,1,0:T(8,128)(2,1)S(1)}, bf16[2,1,512,768]{3,2,1,0:T(8,128)(2,1)}, u32[]{:S(2)}) copy-start(bf16[2,1,512,768]{3,2,1,0:T(8,128)(2,1)} %param.15) | copy-start | bytes 4718596
  632.6 151.0 %collective-permute-start.4 = (bf16[192,1152]{1,0:T(8,128)(2,1)S(1)}, bf16[192,1152]{1,0:T(8,128)(2,1)S(1)}, u32[]{:S(2)}, u32[]{:S(2)}) collective-permute-start(bf16[192,1152]{1,0:T(8,128)(2,1)S(1)} %all_gather.32), channel_id=1, source_target_pairs={{0,1},{1,0},{2,3},{3,2},{4,5},{5,4},{6,7},{7,6},{8,9},{9,8},{10,11... | collective-permute-start | bytes 1327112 | tf_op jit(solution)/shard_map/ppermute | solution.py:195
  783.9 8.5 %copy-start.1 = (bf16[192,3072]{1,0:T(8,128)(2,1)S(1)}, bf16[192,3072]{1,0:T(8,128)(2,1)}, u32[]{:S(2)}) copy-start(bf16[192,3072]{1,0:T(8,128)(2,1)} %param.25) | copy-start | bytes 3538948
Sparse Core Ops, SparseCore 0:
  11.4 59.9 all-gather.8
  74.3 54.5 all-gather.10
  131.8 62.5 all-gather.12
  197.7 62.4 all-gather.14
  287.9 103.8 reduce-scatter.8
  397.6 95.3 reduce-scatter.6
  499.2 124.6 reduce-scatter.4
  630.2 105.9 reduce-scatter.10
  738.1 25.5 all-gather.16
  765.4 24.0 all-gather.18

commit v2 on v1

--- a/solution.py
+++ b/solution.py
@@ -163,6 +163,293 @@
     )(q, k, v, do, lse)
 
 
+MESH = pl.DeviceIdType.MESH
+
+
+def position():
+    return lax.axis_index("fsdp"), lax.axis_index("rep"), lax.axis_index("ctx")
+
+
+def greet(owners, reps):
+    z, r, c = position()
+    barrier = pltpu.get_barrier_semaphore()
+    peers = [{"fsdp": lax.rem(z + j, owners)} for j in range(1, owners)]
+    peers += [{"rep": r ^ j} for j in range(1, reps)]
+    peers += [{"ctx": 1 - c}]
+    for peer in peers:
+        pl.semaphore_signal(barrier, inc=1, device_id=peer, device_id_type=MESH)
+    pl.semaphore_wait(barrier, len(peers))
+
+
+class Copies:
+    def __init__(self, send, recv, local):
+        self.send, self.recv, self.local = send, recv, local
+        self.slots, self.locals = 0, 0
+        self.sent, self.kept = [], []
+
+    def remote(self, src, dst, peer):
+        copy = pltpu.make_async_remote_copy(
+            src_ref=src,
+            dst_ref=dst,
+            send_sem=self.send.at[self.slots],
+            recv_sem=self.recv.at[self.slots],
+            device_id=peer,
+            device_id_type=MESH,
+        )
+        self.slots += 1
+        copy.start()
+        self.sent.append(copy)
+        return copy
+
+    def keep(self, src, dst):
+        copy = pltpu.make_async_copy(src, dst, self.local.at[self.locals])
+        self.locals += 1
+        copy.start()
+        self.kept.append(copy)
+        return copy
+
+    def close(self):
+        for copy in self.sent:
+            copy.wait_send()
+
+
+def slab(i, half):
+    return pl.ds(pl.multiple_of(i * half, 128), half)
+
+
+def gather_kernel(owners, reps, qkv_ref, mix_ref, up_ref, down_ref, small_ref, w_qkv, w_mix, w_up, w_down, w_small, send, recv, kept):
+    z, r, c = position()
+    greet(owners, reps)
+    copies = Copies(send, recv, kept)
+    items = [(mix_ref, w_mix), (up_ref, w_up), (down_ref, w_down)]
+    half = w_qkv.shape[-1] // 3
+    peers_z = [{"fsdp": lax.rem(z + j, owners)} for j in range(1, owners)]
+    origins = [lax.rem(z - j + owners, owners) for j in range(1, owners)]
+    peers_r = [{"rep": r ^ k} for k in range(1, reps)]
+
+    small = [copies.remote(small_ref, w_small.at[z], to) for to in peers_z]
+    first = [
+        [
+            copies.remote(qkv_ref.at[r, :, slab(2 * i + c, half)], w_qkv.at[z, r, :, slab(i, half)], to)
+            for i in range(3)
+        ]
+        for to in peers_z
+    ]
+    rest = [[copies.remote(shard.at[c, r], whole.at[z, c, r], to) for to in peers_z] for shard, whole in items]
+    copies.keep(small_ref, w_small.at[z])
+    for i in range(3):
+        copies.keep(qkv_ref.at[:, :, slab(2 * i + c, half)], w_qkv.at[z, :, :, slab(i, half)])
+    for shard, whole in items:
+        copies.keep(shard, whole.at[z])
+
+    spread = []
+    for arrived, origin in zip(first, origins):
+        for copy in arrived:
+            copy.wait_recv()
+        piece = w_qkv.at[origin, r]
+        spread += [copies.remote(piece, piece, to) for to in peers_r]
+    spread_rest = []
+    for (shard, whole), arrived in zip(items, rest):
+        for copy, origin in zip(arrived, origins):
+            copy.wait_recv()
+            piece = whole.at[origin, c, r]
+            spread_rest.append((whole.at[origin, c], [copies.remote(piece, piece, to) for to in peers_r]))
+    last = []
+    for side, arrived in spread_rest:
+        for copy in arrived:
+            copy.wait_recv()
+        last.append(copies.remote(side, side, {"ctx": 1 - c}))
+    for copy in small + spread + last:
+        copy.wait_recv()
+    copies.close()
+    for copy in copies.kept:
+        copy.wait()
+
+
+def gather_weights(owners, reps, weight_qkv, weight_mix, weight_up, weight_down, small):
+    own, wide = weight_qkv.shape
+
+    def cut(shard):
+        return shard.reshape(2, reps, shard.shape[0] // (2 * reps), shard.shape[1])
+
+    ins = (
+        weight_qkv.reshape(reps, own // reps, wide),
+        cut(weight_mix),
+        cut(weight_up),
+        cut(weight_down),
+        small,
+    )
+    shapes = [(owners, reps, own // reps, wide // 2)] + [(owners,) + x.shape for x in ins[1:]]
+    remotes = (owners - 1) * (4 + 3 + 4 * (reps - 1) + 3)
+    whole = pl.pallas_call(
+        partial(gather_kernel, owners, reps),
+        in_specs=[pl.BlockSpec(memory_space=pl.ANY)] * 5,
+        out_specs=[pl.BlockSpec(memory_space=pl.ANY)] * 5,
+        out_shape=[jax.ShapeDtypeStruct(s, BF16) for s in shapes],
+        scratch_shapes=[
+            pltpu.SemaphoreType.DMA((remotes,)),
+            pltpu.SemaphoreType.DMA((remotes,)),
+            pltpu.SemaphoreType.DMA((7,)),
+        ],
+        compiler_params=pltpu.CompilerParams(collective_id=1, has_side_effects=True),
+        name="gather_weights",
+    )(*ins)
+    return (
+        whole[0].reshape(owners * own, wide // 2),
+        whole[1].reshape(owners * own, -1),
+        whole[2].reshape(owners * own, -1),
+        whole[3].reshape(owners * weight_down.shape[0], -1),
+        whole[4],
+    )
+
+
+def add_blocks(out, parts, dtype):
+    lead = out.shape[:-2]
+    count = 1
+    for n in lead:
+        count *= n
+
+    def body(i, _):
+        at = []
+        for n in reversed(lead):
+            at.append(lax.rem(i, n))
+            i = lax.div(i, n)
+        at = tuple(reversed(at))
+        terms = [p[at].astype(F32) for p in parts]
+        while len(terms) > 1:
+            terms = [a + b for a, b in zip(terms[::2], terms[1::2])]
+        out[at] = terms[0].astype(dtype)
+        return 0
+
+    lax.fori_loop(0, count, body, 0)
+
+
+def reduce_kernel(owners, reps, *refs):
+    z, r, c = position()
+    n = 4
+    ins, vec = refs[:n], refs[n]
+    outs, vec_out = refs[n + 1 : 2 * n + 1], refs[2 * n + 1]
+    refs = refs[2 * n + 2 :]
+    sums, from_core, from_reps, from_owners, finals = (refs[i * n : (i + 1) * n] for i in range(5))
+    v_core, v_reps, v_mid, v_late, v_owners, send, recv, kept = refs[5 * n :]
+    greet(owners, reps)
+    copies = Copies(send, recv, kept)
+    peers_z = [lax.rem(z + j, owners) for j in range(1, owners)]
+    peers_r = [r ^ k for k in range(1, reps)]
+    other = {"ctx": 1 - c}
+    halved = [len(x.shape) == 5 for x in ins]
+
+    loads, cores = [], []
+    v_first = copies.remote(vec, v_core, other)
+    for x, mine, theirs, split in zip(ins, sums, from_core, halved):
+        if split:
+            cores.append(copies.remote(x.at[:, 1 - c], theirs, other))
+            loads.append(copies.keep(x.at[:, c], mine))
+        else:
+            cores.append(None)
+            loads.append(copies.keep(x, mine))
+    v_first.wait_recv()
+    v_mid[...] = vec[...] + v_core[...]
+    v_second = [copies.remote(v_mid, v_reps.at[k], {"rep": p}) for k, p in enumerate(peers_r)]
+    seconds = []
+    for mine, theirs, load, core, gets in zip(sums, from_core, loads, cores, from_reps):
+        load.wait()
+        if core is not None:
+            core.wait_recv()
+            add_blocks(mine, [mine, theirs], BF16)
+        seconds.append([copies.remote(mine.at[:, p], gets.at[k], {"rep": p}) for k, p in enumerate(peers_r)])
+    for copy in v_second:
+        copy.wait_recv()
+    v_late[...] = (v_mid[...] + v_reps[0]) + (v_reps[1] + v_reps[2])
+    v_third = [copies.remote(v_late.at[p], v_owners.at[j], {"fsdp": p}) for j, p in enumerate(peers_z)]
+    thirds = []
+    for mine, arrived, gets, at_owner in zip(sums, seconds, from_reps, from_owners):
+        for copy in arrived:
+            copy.wait_recv()
+        add_blocks(gets.at[0], [mine.at[:, r]] + [gets.at[k] for k in range(reps - 1)], BF16)
+        thirds.append([copies.remote(gets.at[0, p], at_owner.at[j], {"fsdp": p}) for j, p in enumerate(peers_z)])
+    fourths = []
+    for arrived, gets, at_owner, final in zip(thirds, from_reps, from_owners, finals):
+        for copy in arrived:
+            copy.wait_recv()
+        terms = [gets[0, z].astype(F32)] + [at_owner[j].astype(F32) for j in range(owners - 1)]
+        while len(terms) > 1:
+            terms = [a + b for a, b in zip(terms[::2], terms[1::2])]
+        final[c, r] = terms[0].astype(BF16)
+        piece = final.at[c, r]
+        fourths.append([copies.remote(piece, piece, {"rep": p}) for p in peers_r])
+    for copy in v_third:
+        copy.wait_recv()
+    vec_out[...] = (v_late[z] + v_owners[0]) + (v_owners[1] + v_owners[2])
+    fifths = []
+    for arrived, final in zip(fourths, finals):
+        for copy in arrived:
+            copy.wait_recv()
+        fifths.append(copies.remote(final.at[c], final.at[c], other))
+    for copy, final, out, split in zip(fifths, finals, outs, halved):
+        copy.wait_recv()
+        if split:
+            for k in range(2):
+                for j in range(reps):
+                    out[k, j] = final[k, j].astype(F32)
+        else:
+            half = final.shape[-1] // 3
+            for k in range(2):
+                for j in range(reps):
+                    whole = final[k, j].astype(F32)
+                    for i in range(3):
+                        out[j, :, (2 * i + k) * half : (2 * i + k + 1) * half] = whole[:, i * half : (i + 1) * half]
+    copies.close()
+
+
+def reduce_grads(owners, reps, g_wdown, g_wup, g_wmix, g_wqkv, vectors):
+    def cut(grad):
+        rows = grad.shape[0] // (owners * 2 * reps)
+        return grad.reshape(owners, 2, reps, rows, grad.shape[1])
+
+    own = g_wqkv.shape[0] // owners
+    ins = [cut(g_wdown), cut(g_wup), cut(g_wmix), g_wqkv.reshape(owners, reps, own // reps, g_wqkv.shape[1])]
+    pieces = [x.shape[-2:] for x in ins]
+    outs = [(2, reps) + p for p in pieces[:3]] + [(reps, pieces[3][0], 2 * pieces[3][1])]
+    spread = [(owners, reps) + p for p in pieces]
+    scratch = [pltpu.VMEM(s, BF16) for s in spread]
+    scratch += [pltpu.VMEM(s, BF16) for s in spread[:3]] + [pltpu.VMEM((8, 128), BF16)]
+    scratch += [pltpu.VMEM((reps - 1, owners) + p, BF16) for p in pieces]
+    scratch += [pltpu.VMEM((owners - 1,) + p, BF16) for p in pieces]
+    scratch += [pltpu.VMEM((2, reps) + p, BF16) for p in pieces]
+    block = vectors.shape[1:]
+    scratch += [
+        pltpu.VMEM((owners,) + block, F32),
+        pltpu.VMEM((reps - 1, owners) + block, F32),
+        pltpu.VMEM((owners,) + block, F32),
+        pltpu.VMEM((owners,) + block, F32),
+        pltpu.VMEM((owners - 1,) + block, F32),
+    ]
+    remotes = 3 + 4 * 2 * (reps - 1) + 4 * (owners - 1) + 4 + 1 + (reps - 1) + (owners - 1)
+    scratch += [
+        pltpu.SemaphoreType.DMA((remotes,)),
+        pltpu.SemaphoreType.DMA((remotes,)),
+        pltpu.SemaphoreType.DMA((4,)),
+    ]
+    vmem = pl.BlockSpec(memory_space=pltpu.VMEM)
+    o_wdown, o_wup, o_wmix, o_wqkv, o_vec = pl.pallas_call(
+        partial(reduce_kernel, owners, reps),
+        in_specs=[pl.BlockSpec(memory_space=pl.ANY)] * 4 + [vmem],
+        out_specs=[vmem] * 5,
+        out_shape=[jax.ShapeDtypeStruct(s, F32) for s in outs] + [jax.ShapeDtypeStruct(block, F32)],
+        scratch_shapes=scratch,
+        compiler_params=pltpu.CompilerParams(collective_id=2, has_side_effects=True, vmem_limit_bytes=60 << 20),
+        name="reduce_grads",
+    )(*ins, vectors)
+    return (
+        o_wdown.reshape(-1, g_wdown.shape[1]),
+        o_wup.reshape(-1, g_wup.shape[1]),
+        o_wmix.reshape(-1, g_wmix.shape[1]),
+        o_wqkv.reshape(own, -1),
+        o_vec,
+    )
+
+
 def local(
     inputs,
     weight_qkv,
@@ -204,28 +491,33 @@
     def columns(x, axis, which):
         return lax.dynamic_slice_in_dim(x, which * half, half, axis)
 
-    flat = jnp.concatenate(
-        [bias_query, bias_value, bias_mix, gain_attn, shift_attn, gain_mlp, shift_mlp, bias_down, bias_up]
+    direct = own % (16 * reps) == 0 and owners == 4 and reps == 4
+    rows8 = jnp.stack(
+        [bias_query, bias_value, bias_mix, gain_attn, shift_attn, gain_mlp, shift_mlp, bias_down]
     )
-    small = lax.all_gather(flat.reshape(1, -1), "fsdp", axis=0, tiled=True).astype(F32)
-    b_query, b_value, b_mix, g_attn, s_attn, g_mlp, s_mlp, b_down = (
-        small[:, i * own : (i + 1) * own].reshape(-1) for i in range(8)
-    )
-    b_up = small[:, 8 * own :].reshape(-1)
-
-    part = own // reps
-    mine = lax.dynamic_slice_in_dim(weight_qkv, rep * part, part, 0)
-    mine = jnp.concatenate([columns(mine[:, i * width : (i + 1) * width], 1, ctx) for i in range(3)], axis=1)
-    w_qkv = lax.all_gather(mine, ("fsdp", "rep"), axis=0, tiled=True)
-
-    def gather(shard):
-        piece = shard.shape[0] // (2 * reps)
-        mine = lax.dynamic_slice_in_dim(shard, (rep * 2 + ctx) * piece, piece, 0)
-        return lax.all_gather(mine, ("fsdp", "rep", "ctx"), axis=0, tiled=True)
-
-    w_mix = gather(weight_mix)
-    w_up = gather(weight_up)
-    w_down = gather(weight_down)
+    small = jnp.concatenate([rows8, bias_up.reshape(-1, own), jnp.zeros((4, own), BF16)], axis=0)
+    if direct:
+        w_qkv, w_mix, w_up, w_down, small = gather_weights(
+            owners, reps, weight_qkv, weight_mix, weight_up, weight_down, small
+        )
+    else:
+        part = own // reps
+        mine = lax.dynamic_slice_in_dim(weight_qkv, rep * part, part, 0)
+        mine = jnp.concatenate([columns(mine[:, i * width : (i + 1) * width], 1, ctx) for i in range(3)], axis=1)
+        w_qkv = lax.all_gather(mine, ("fsdp", "rep"), axis=0, tiled=True)
+
+        def gather(shard):
+            piece = shard.shape[0] // (2 * reps)
+            mine = lax.dynamic_slice_in_dim(shard, (rep * 2 + ctx) * piece, piece, 0)
+            return lax.all_gather(mine, ("fsdp", "rep", "ctx"), axis=0, tiled=True)
+
+        w_mix = gather(weight_mix)
+        w_up = gather(weight_up)
+        w_down = gather(weight_down)
+        small = lax.all_gather(small, "fsdp")
+    small = small.astype(F32)
+    b_query, b_value, b_mix, g_attn, s_attn, g_mlp, s_mlp, b_down = (small[:, i].reshape(-1) for i in range(8))
+    b_up = small[:, 8:-4].reshape(-1)
 
     tokens = inputs[:, 0].astype(F32)
     normal_one, inverse_one = norm_stats(tokens)
@@ -280,35 +572,43 @@
     g_sattn = jnp.sum(d_first, axis=(0, 1))
     d_tokens = d_middle + norm_back(d_first, normal_one, inverse_one, g_attn)
 
-    def reduce(grad):
-        piece = lax.psum_scatter(
-            grad.astype(BF16), ("fsdp", "rep", "ctx"), scatter_dimension=0, tiled=True
-        )
-        return lax.all_gather(piece, ("rep", "ctx"), axis=0, tiled=True).astype(F32)
-
-    o_wdown = reduce(g_wdown)
-    o_wup = reduce(g_wup)
-    o_wmix = reduce(g_wmix)
-    piece = lax.psum_scatter(g_wqkv.astype(BF16), ("fsdp", "rep"), scatter_dimension=0, tiled=True)
-    piece = lax.all_gather(piece, "rep", axis=0, tiled=True)
-    other = swap(piece)
-    low, high = jnp.where(ctx == 0, piece, other), jnp.where(ctx == 0, other, piece)
-    o_wqkv = jnp.concatenate(
-        [t for i in range(3) for t in (low[:, i * half : (i + 1) * half], high[:, i * half : (i + 1) * half])],
-        axis=1,
-    ).astype(F32)
-
     zeros = jnp.zeros((width,), F32)
 
     def place(v):
         return lax.dynamic_update_slice_in_dim(zeros, v, ctx * half, 0)
 
     vectors = (place(g_bquery), place(g_bvalue), g_bmix, g_gattn, g_sattn, g_gmlp, g_smlp, g_bdown)
-    stacked = jnp.concatenate([v.reshape(owners, own) for v in vectors] + [g_bup.reshape(owners, -1)], axis=1)
-    summed = lax.psum(stacked, ("rep", "fsdp", "ctx"))
-    summed = lax.dynamic_slice_in_dim(summed, lax.axis_index("fsdp"), 1, 0)[0]
-    o_bq, o_bv, o_bmix, o_ga, o_sa, o_gm, o_sm, o_bd = (summed[i * own : (i + 1) * own] for i in range(8))
-    o_bup = summed[8 * own :]
+    stacked = jnp.concatenate(
+        [jnp.stack([v.reshape(owners, own) for v in vectors], axis=1), g_bup.reshape(owners, -1, own), jnp.zeros((owners, 4, own), F32)],
+        axis=1,
+    )
+    if direct:
+        o_wdown, o_wup, o_wmix, o_wqkv, summed = reduce_grads(
+            owners, reps, g_wdown.astype(BF16), g_wup.astype(BF16), g_wmix.astype(BF16), g_wqkv.astype(BF16), stacked
+        )
+    else:
+
+        def reduce(grad):
+            piece = lax.psum_scatter(
+                grad.astype(BF16), ("fsdp", "rep", "ctx"), scatter_dimension=0, tiled=True
+            )
+            return lax.all_gather(piece, ("rep", "ctx"), axis=0, tiled=True).astype(F32)
+
+        o_wdown = reduce(g_wdown)
+        o_wup = reduce(g_wup)
+        o_wmix = reduce(g_wmix)
+        piece = lax.psum_scatter(g_wqkv.astype(BF16), ("fsdp", "rep"), scatter_dimension=0, tiled=True)
+        piece = lax.all_gather(piece, "rep", axis=0, tiled=True)
+        other = swap(piece)
+        low, high = jnp.where(ctx == 0, piece, other), jnp.where(ctx == 0, other, piece)
+        o_wqkv = jnp.concatenate(
+            [t for i in range(3) for t in (low[:, i * half : (i + 1) * half], high[:, i * half : (i + 1) * half])],
+            axis=1,
+        ).astype(F32)
+        summed = lax.psum(stacked, ("rep", "fsdp", "ctx"))
+        summed = lax.dynamic_index_in_dim(summed, lax.axis_index("fsdp"), 0, keepdims=False)
+    o_bq, o_bv, o_bmix, o_ga, o_sa, o_gm, o_sm, o_bd = (summed[i] for i in range(8))
+    o_bup = summed[8:-4].reshape(-1)
     return (
         result[:, None],
         d_tokens[:, None],

time: 809 us -> 427 us (0.53)
  waiting for transfers between devices: 478 us -> 4.39 us
  Pallas kernels: 57.3 us -> 273 us
  blocking collectives: 73.2 us -> 0 us
  between operations: 15.1 us -> 1.59 us
  matrix products: 108 us -> 95.8 us
  other arithmetic: 31.1 us -> 20.9 us
  starting transfers between devices: 10.8 us -> 2.02 us
    reduce_scatter x4 -> x0, waiting for transfers between devices: 311 us -> none  [the longest x3 198 us: reduce(): lax.psum_scatter(grad.astype(BF16), ('fsdp', 'rep', 'ctx'), scatter_dimen...]
    pallas_call x0 -> x2, Pallas kernels: none -> 215 us  [the longest x1 114 us: reduce_grads(): pl.pallas_call(partial(reduce_kernel, owners, reps), in_specs=[pl.BlockSp...]
    all_gather x6 -> x0, waiting for transfers between devices: 163 us -> none  [the longest x3 133 us: gather(): return lax.all_gather(mine, ('fsdp', 'rep', 'ctx'), axis=0, tiled=True)]
    psum x1 -> x0, blocking collectives: 41.2 us -> none  [local(): summed = lax.psum(stacked, ('rep', 'fsdp', 'ctx'))]
    all_gather x3 -> x0, blocking collectives: 32 us -> none  [the longest x1 11.6 us: local(): lax.all_gather(flat.reshape(1, -1), 'fsdp', axis=0, tiled=True).astype(F32)]
  transfers between devices with their start and end apart: 15 -> 4, of which waited for: 10 -> 2; matrix products, arithmetic and copies ran while one was open for 16% -> 6% of each run, Pallas kernels for 7% -> 0%
where the time goes in v2:
time: 427 us; the launch traced here: 420 us
  Pallas kernels  273 us (64%)
  matrix products  95.8 us (22%)
  local copies, waits for them, and re-layouts  23.1 us (5%)
  other arithmetic  20.9 us (5%)
  waiting for transfers between devices  4.39 us (1%)
    pallas_call x1, Pallas kernels, reduce_grads(): pl.pallas_call(partial(reduce_kernel, owners, reps), in_specs=[pl.BlockSp...  114 us
    pallas_call x1, Pallas kernels, gather_weights(): pl.pallas_call(partial(gather_kernel, owners, reps), in_specs=[pl.BlockSp...  101 us
    dot_general x4, matrix products, outer_sum(): return jnp.einsum('sri,srj->ij', left, right, preferred_element_type=F32)  35.3 us
    pallas_call x1, Pallas kernels, attention_backward(): pl.pallas_call(partial(attention_backward_kernel, factor, size), grid=(mb...  32 us
    dot_general x4, matrix products, project_back(): jnp.einsum('srj,ij->sri', grad_rows, weight, preferred_element_type=F32)  30.3 us
    dot_general x4, matrix products, project(): return jnp.einsum('sri,ij->srj', left, weight, preferred_element_type=F32)  30.2 us
    pallas_call x1, Pallas kernels, attention_forward(): pl.pallas_call(partial(attention_forward_kernel, factor, size), grid=(mbs...  25.8 us
  transfers between devices with their start and end apart: 4, of which 2 were waited for; matrix products, arithmetic and copies ran while one was open for 6% of the time, Pallas kernels for 0%

profile of v2, /device:TPU:1, one launch (start us, length us, event | category | flops | bytes accessed | tf_op | source)
XLA Modules:
  0.0 420.4 jit_solution(13300122971234533135)
XLA Ops:
  0.6 0.7 stack.24
  1.3 0.7 stack.25
  2.0 0.7 stack.26
  2.6 0.7 stack.27
  3.3 0.7 stack.28
  3.9 0.7 stack.29
  4.6 0.7 stack.30
  5.3 0.7 stack.31
  5.9 0.8 reshape.141
  6.7 1.8 convert_reduce_fusion.2
  8.5 2.0 fusion.27
  10.6 1.2 concatenate.27.small_ref
  11.8 100.7 %gather_weights.1 = (bf16[4,4,48,1152]{3,2,1,0:T(8,128)(2,1)}, bf16[4,2,4,24,768]{4,3,2,1,0:T(8,128)(2,1)}, bf16[4,2,4,24,3072]{4,3,2,1,0:T(8,128)(2,1)}, bf16[4...) custom-call(bf16[4,48,2304]{2,1,0:T(8,128)(2,1)} %bitcast.140, bf16[2,4,24,768]{3,2,1,0:T(8,128)(2,1)} %bitcast.142, ...), custom_call_target="tpu_custom_call" | custom-call | tf_op jit(solution)/shard_map/gather_weights/pallas_call | solution.py:284
  112.4 0.8 convert_element_type.72
  113.5 0.6 fusion.20
  114.2 1.0 collective-permute-start
  115.5 2.9 collective-permute-done
  118.3 6.8 %fusion.34 = f32[2,1024,1152]{2,1,0:T(8,128)S(1)} fusion(bf16[768,1152,1]{1,0,2:T(8,128)(2,1)} %bitcast.159, bf16[2,512,768]{2,1,0:T(8,128)(2,1)} %collective-permute-done, bf16[2,512,768]{2,1,0:T(8,128)(2,1)S(1)} %fusion.20, pred[]{:T(512)S(6)} %eq.2), kind=kOutput, calls=%fused_computation.68 | convolution fusion | flops 3638034432 | bytes 14352385 | tf_op jit(solution)/shard_map/sri,ij->srj/dot_general | solution.py:37
  125.3 1.7 fusion.29
  127.0 25.8 %attention_forward.1 = (bf16[2,1024,384]{2,1,0:T(8,128)(2,1)S(1)}, f32[2,3,8,1024]{3,2,1,0:T(8,128)S(1)}) custom-call(bf16[2,1024,384]{2,1,0:T(8,128)(2,1)S(1)} %get-tuple-element.80.q_ref, bf16[2,1024,384]{2,1,0:T(8,128)(2,1)S(1)} %slice.112.k_ref, bf16[2,1024,384]{2,1,0:T(8,128)(2,1)} %get-tuple-element.79.v_ref), custom_call_target="tpu_custom_call" | custom-call | flops 8053063680 | bytes 6291456 | tf_op jit(solution)/shard_map/attention_forward/pallas_call | solution.py:93
  154.0 1.5 collective-permute-done.1
  155.5 3.4 fusion.43
  159.5 8.2 %fusion.35 = f32[2,512,3072]{2,1,0:T(8,128)} fusion(bf16[768,3072,1]{1,0,2:T(8,128)(2,1)S(1)} %bitcast.153, f32[2,512,768]{2,1,0:T(8,128)S(1)} %get-tuple-element.95, f32[768]{0:T(1024)S(1)} %add.138, f32[768]{0:T(1024)S(1)} %mul.168, f32[2,512]{1,0:T(2,128)S(1)} %add_rsqrt_fusion, f32[2,512]{1,0:T(2,128)S(1)} %broadcast_multiply_fusion.4), kind=kOutput, calls=%fused_computation.69 | convolution fusion | flops 4835770368 | bytes 20461568 | tf_op jit(solution)/shard_map/sri,ij->srj/dot_general | solution.py:37
  167.7 12.3 %bitcast_convert_fusion.1 = bf16[3072,768]{1,0:T(8,128)(2,1)} fusion(bf16[2,1,512,768]{3,2,1,0:T(8,128)(2,1)S(1)} %copy-done.10, f32[2,512,3072]{2,1,0:T(8,128)} %fusion.35, f32[3072]{0:T(1024)S(1)} %add.141), kind=kOutput, calls=%fused_computation.17 | convolution fusion | flops 4865654784 | bytes 18886656 | tf_op jit(solution)/shard_map/sri,srj->ij/dot_general | solution.py:33
  180.0 16.3 %convert_reduce_fusion = (f32[3072]{0:T(1024)S(1)}, bf16[2,512,3072]{2,1,0:T(8,128)(2,1)}) fusion(f32[2,512,3072]{2,1,0:T(8,128)} %fusion.35, f32[3072]{0:T(1024)S(1)} %add.141, bf16[3072,768,1]{1,0,2:T(8,128)(2,1)S(1)} %bitcast.157, bf16[2,1,512,768]{3,2,1,0:T(8,128)(2,1)S(1)} %copy-done.10), kind=kOutput, calls=%fused_computation.14 | convolution fusion | flops 4904186880 | bytes 25190400 | tf_op jit(solution)/shard_map/srj,ij->sri/dot_general | solution.py:41
  196.3 11.8 %fusion.33 = bf16[2,1,512,768]{3,2,1,0:T(8,128)(2,1)} fusion(f32[768]{0:T(1024)S(1)} %add.147, f32[2,512,768]{2,1,0:T(8,128)S(1)} %get-tuple-element.95, bf16[3072,768,1]{1,0,2:T(8,128)(2,1)S(1)} %bitcast.158, f32[2,512,3072]{2,1,0:T(8,128)} %fusion.35, f32[3072]{0:T(1024)S(1)} %add.141), kind=kOutput, calls=%fused_computation.67 | convolution fusion | flops 4865654784 | bytes 22035456 | tf_op jit(solution)/shard_map/sri,ij->srj/dot_general | solution.py:37
  208.2 8.3 %multiply_reduce_fusion = (f32[768]{0:T(1024)S(1)}, f32[2,512]{1,0:T(2,128)S(1)}, f32[2,512]{1,0:T(2,128)S(1)}, f32[768]{0:T(1024)S(1)}, f32[2,512,768]{2,1,0:T(8,128)S(1)}) fusion(f32[2,512,768]{2,1,0:T(8,128)S(1)} %get-tuple-element.95, f32[2,512]{1,0:T(2,128)S(1)} %add_rsqrt_fusion, f32[2,512]{1,0:T(2,128)S(1)} %broadcast_multiply_fusion.4, ...), kind=kOutput, calls=%fused_computation.48 | convolution fusion | flops 4838912000 | bytes 17327104 | tf_op jit(solution)/shard_map/srj,ij->sri/dot_general | solution.py:41
  216.5 1.8 convert_reduce_fusion.3
  218.3 1.4 convolution_convert_fusion
  220.3 8.0 %bitcast_convert_fusion = bf16[768,3072]{1,0:T(8,128)(2,1)} fusion(bf16[2,512,3072]{2,1,0:T(8,128)(2,1)S(1)} %bitcast.164, f32[2,512,768]{2,1,0:T(8,128)S(1)} %get-tuple-element.95, f32[768]{0:T(1024)S(1)} %add.138, f32[768]{0:T(1024)S(1)} %mul.168, f32[2,512]{1,0:T(2,128)S(1)} %add_rsqrt_fusion, f32[2,512]{1,0:T(2,128)S(1)} %broadcast_multiply_fusion.4), kind=kOutput, calls=%fused_computation.16 | convolution fusion | flops 4838129664 | bytes 14170112 | tf_op jit(solution)/shard_map/sri,srj->ij/dot_general | solution.py:33
  228.3 1.6 maximum_select_fusion.2.do_ref
  229.9 32.0 %attention_backward.1 = (bf16[2,1024,384]{2,1,0:T(8,128)(2,1)S(1)}, bf16[2,1024,384]{2,1,0:T(8,128)(2,1)S(1)}, bf16[2,1024,384]{2,1,0:T(8,128)(2,1)S(1)}) custom-call(bf16[2,1024,384]{2,1,0:T(8,128)(2,1)} %copy-done.1, bf16[2,1024,384]{2,1,0:T(8,128)(2,1)} %copy-done, bf16[2,1024,384]{2,1,0:T(8,128)(2,1)} %get-tuple-element.79.v_ref, ...), custom_call_target="tpu_custom_call" | custom-call | flops 20132659200 | bytes 11010048 | tf_op jit(solution)/shard_map/attention_backward/pallas_call | solution.py:151
  262.8 0.8 copy-done.22
  263.6 4.3 %fusion.44 = f32[2,1024,768]{2,1,0:T(8,128)S(1)} fusion(bf16[2,1024,1152]{2,1,0:T(8,128)(2,1)S(1)} %constant_dynamic-update-slice_fusion, bf16[768,1152,1]{1,0,2:T(8,128)(2,1)S(1)} %bitcast.160), kind=kOutput, calls=%fused_computation.101 | convolution fusion | flops 3623878656 | bytes 12779520 | tf_op jit(solution)/shard_map/srj,ij->sri/dot_general | solution.py:41
  267.9 1.3 dynamic-slice_convert_fusion
  269.6 5.0 %bitcast_convert_fusion.2 = bf16[768,768]{1,0:T(8,128)(2,1)} fusion(bf16[2,512,384]{2,1,0:T(8,128)(2,1)} %collective-permute-done.1, bf16[2,512,384]{2,1,0:T(8,128)(2,1)S(1)} %copy-done.12, pred[]{:T(512)S(6)} %eq.2, f32[2,512,768]{2,1,0:T(8,128)S(1)} %get-tuple-element.77), kind=kOutput, calls=%fused_computation.61 | convolution fusion | flops 1216413696 | bytes 5898241 | tf_op jit(solution)/shard_map/sri,srj->ij/dot_general | solution.py:33
  276.3 10.0 %fusion.18 = bf16[768,1152]{1,0:T(8,128)(2,1)} fusion(bf16[2,1024,1152]{2,1,0:T(8,128)(2,1)} %copy-done.14, bf16[2,512,768]{2,1,0:T(8,128)(2,1)} %collective-permute-done, bf16[2,512,768]{2,1,0:T(8,128)(2,1)} %copy-done.9, pred[]{:T(512)S(6)} %eq.2), kind=kOutput, calls=%fused_computation.31 | convolution fusion | flops 3638919168 | bytes 9633793 | tf_op jit(solution)/shard_map/sri,srj->ij/dot_general | solution.py:33
  286.3 4.8 %fusion.26 = (f32[768]{0:T(1024)S(1)}, f32[2,512]{1,0:T(2,128)S(1)}, f32[2,512]{1,0:T(2,128)S(1)}, f32[768]{0:T(1024)S(1)}, f32[2,512,768]{2,1,0:T(8,128)}) fusion(bf16[2,1,512,768]{3,2,1,0:T(8,128)(2,1)S(1)} %copy-done.3, f32[2,512]{1,0:T(2,128)S(1)} %copy-done.19, f32[2,512]{1,0:T(2,128)S(1)} %copy-done.16, f32[768]{0:T(1024)S(1)} %copy-done.21, ...), kind=kLoop, calls=%fused_computation.39 | loop fusion | flops 9433600 | bytes 9462788 | tf_op jit(solution)/shard_map/reduce_sum | solution.py:571
  291.3 1.3 concatenate.35.refs_4_
  292.6 114.2 %reduce_grads.1 = (f32[2,4,96,768]{3,2,1,0:T(8,128)}, f32[2,4,24,3072]{3,2,1,0:T(8,128)}, f32[2,4,24,768]{3,2,1,0:T(8,128)}, f32[4,48,2304]{2,1,0:T(8,128)}, f32[16,192]{1,0:T(8,128)}) custom-call(bf16[4,2,4,96,768]{4,3,2,1,0:T(8,128)(2,1)} %bitcast.131, bf16[4,2,4,24,3072]{4,3,2,1,0:T(8,128)(2,1)} %bitcast.132, bf16[4,2,4,24,768]{4,3,2,1,0:T(8,128)(2,1)} %bitcast.137, ...), custom_call_target="tpu_custom_call" | custom-call | tf_op jit(solution)/shard_map/reduce_grads/pallas_call | solution.py:435
  406.8 0.7 slice.83
  407.5 1.6 fusion.42
  409.1 0.7 reshape.154
  409.8 4.6 %fusion.25 = f32[2,1,512,768]{3,2,1,0:T(8,128)} fusion(f32[2,512,768]{2,1,0:T(8,128)} %copy-done.4, f32[2,512,768]{2,1,0:T(8,128)} %get-tuple-element.78, bf16[2,1,512,768]{3,2,1,0:T(8,128)(2,1)S(1)} %copy-done.3, f32[2,512]{1,0:T(2,128)S(1)} %broadcast_multiply_fusion, f32[2,512]{1,0:T(2,128)S(1)} %broadcast_multiply_fusion.1, f32[768]{0:T(1024)S(1)} %copy-done.21, ...), kind=kLoop, calls=%fused_computation.38 | loop fusion | flops 7077888 | bytes 11029504
  414.4 1.2 copy.49
  415.8 0.8 copy.50
  417.1 1.4 copy.51
  418.5 1.4 copy.52
  (111 shorter events, 6.7 us)
Async XLA Ops:
  6.7 106.8 %copy-start.2 = (bf16[2,1,512,768]{3,2,1,0:T(8,128)(2,1)S(1)}, bf16[2,1,512,768]{3,2,1,0:T(8,128)(2,1)}, u32[]{:S(2)}) copy-start(bf16[2,1,512,768]{3,2,1,0:T(8,128)(2,1)} %param.15) | copy-start | bytes 4718596
  8.5 105.6 %copy-start.15 = (f32[2,512]{1,0:T(2,128)}, f32[2,512]{1,0:T(2,128)S(1)}, u32[]{:S(2)}) copy-start(f32[2,512]{1,0:T(2,128)S(1)} %broadcast_multiply_fusion.5) | copy-start | bytes 12292
  10.5 103.6 %copy-start.18 = (f32[2,512]{1,0:T(2,128)}, f32[2,512]{1,0:T(2,128)S(1)}, u32[]{:S(2)}) copy-start(f32[2,512]{1,0:T(2,128)S(1)} %add_rsqrt_fusion.1) | copy-start | bytes 12292
  113.4 11.7 %copy-start.20 = (f32[768]{0:T(1024)}, f32[768]{0:T(1024)S(1)}, u32[]{:S(2)}) copy-start(f32[768]{0:T(1024)S(1)} %mul.159) | copy-start | bytes 9220
  114.1 11.0 %copy-start.9 = (bf16[2,512,768]{2,1,0:T(8,128)(2,1)}, bf16[2,512,768]{2,1,0:T(8,128)(2,1)S(1)}, u32[]{:S(2)}) copy-start(bf16[2,512,768]{2,1,0:T(8,128)(2,1)S(1)} %fusion.20) | copy-start | bytes 4718596
  114.2 4.2 collective-permute-start
  125.3 1.7 copy-start
  127.0 25.8 %copy-start.1 = (bf16[2,1024,384]{2,1,0:T(8,128)(2,1)}, bf16[2,1024,384]{2,1,0:T(8,128)(2,1)S(1)}, u32[]{:S(2)}) copy-start(bf16[2,1024,384]{2,1,0:T(8,128)(2,1)S(1)} %get-tuple-element.80.q_ref) | copy-start | bytes 4718596
  152.8 0.8 copy-start.17
  153.0 5.9 %copy-start.11 = (bf16[2,512,384]{2,1,0:T(8,128)(2,1)}, bf16[2,512,384]{2,1,0:T(8,128)(2,1)S(1)}, u32[]{:S(2)}) copy-start(bf16[2,512,384]{2,1,0:T(8,128)(2,1)S(1)} %get-tuple-element.84) | copy-start | bytes 2359300
  153.0 2.5 collective-permute-start.1
  155.5 4.0 slice-start
  155.5 4.0 slice-start.1
  159.5 8.2 %copy-start.10 = (bf16[2,1,512,768]{3,2,1,0:T(8,128)(2,1)S(1)}, bf16[2,1,512,768]{3,2,1,0:T(8,128)(2,1)}, u32[]{:S(2)}) copy-start(bf16[2,1,512,768]{3,2,1,0:T(8,128)(2,1)} %param.29) | copy-start | bytes 4718596
  159.5 20.5 %slice-start.2 = ((s8[4718592]{0:T(1024)(128)(4,1)}), s8[4194304]{0:T(1024)(128)(4,1)S(1)}, s32[]{:S(2)}) async-start(s8[4718592]{0:T(1024)(128)(4,1)} %bitcast.155), calls=%async_computation.2 | async-start | bytes 8388608
  167.7 12.3 %slice-start.3 = ((s8[4718592]{0:T(1024)(128)(4,1)}), s8[524288]{0:T(1024)(128)(4,1)S(1)}, s32[]{:S(2)}) async-start(s8[4718592]{0:T(1024)(128)(4,1)} %bitcast.155), calls=%async_computation.3 | async-start | bytes 1048576
  196.3 24.0 %slice-start.4 = ((s8[6291456]{0:T(1024)(128)(4,1)}), s8[2097152]{0:T(1024)(128)(4,1)S(1)}, s32[]{:S(2)}) async-start(s8[6291456]{0:T(1024)(128)(4,1)} %bitcast.163), calls=%async_computation.4 | async-start | bytes 4194304
  208.2 12.2 %slice-start.5 = ((s8[6291456]{0:T(1024)(128)(4,1)}), s8[4194304]{0:T(1024)(128)(4,1)S(1)}, s32[]{:S(2)}) async-start(s8[6291456]{0:T(1024)(128)(4,1)} %bitcast.163), calls=%async_computation.5 | async-start | bytes 8388608
  216.5 1.8 copy-start.23
  218.2 51.2 %copy-start.4 = (f32[2,512,768]{2,1,0:T(8,128)}, f32[2,512,768]{2,1,0:T(8,128)S(1)}, u32[]{:S(2)}) copy-start(f32[2,512,768]{2,1,0:T(8,128)S(1)} %get-tuple-element.77) | copy-start | bytes 9437188
  219.9 8.4 %collective-permute-start.2 = (bf16[2,512,384]{2,1,0:T(8,128)(2,1)S(1)}, bf16[2,512,384]{2,1,0:T(8,128)(2,1)S(1)}, u32[]{:S(2)}, u32[]{:S(2)}) collective-permute-start(bf16[2,512,384]{2,1,0:T(8,128)(2,1)S(1)} %get-tuple-element.83), channel_id=1, source_target_pairs={{0,1},{1,0},{2,3},{3,2},{4,5},{5,4},{6,7},{7,6},{8,9},{9,8},{10,11... | collective-permute-start | bytes 2359304 | tf_op jit(solution)/shard_map/ppermute | solution.py:482
  262.1 1.5 copy-start.22
  263.6 4.3 %copy-start.14 = (bf16[2,1024,1152]{2,1,0:T(8,128)(2,1)}, bf16[2,1024,1152]{2,1,0:T(8,128)(2,1)S(1)}, u32[]{:S(2)}) copy-start(bf16[2,1024,1152]{2,1,0:T(8,128)(2,1)S(1)} %constant_dynamic-update-slice_fusion) | copy-start | bytes 14155780
  267.9 6.7 %copy-start.5 = (f32[2,1024,768]{2,1,0:T(8,128)}, f32[2,1024,768]{2,1,0:T(8,128)S(1)}, u32[]{:S(2)}) copy-start(f32[2,1024,768]{2,1,0:T(8,128)S(1)} %fusion.44) | copy-start | bytes 18874372
  267.9 1.7 copy-start.12
  269.2 17.0 %collective-permute-start.3 = (bf16[2,512,768]{2,1,0:T(8,128)(2,1)}, bf16[2,512,768]{2,1,0:T(8,128)(2,1)}, u32[]{:S(2)}, u32[]{:S(2)}) collective-permute-start(bf16[2,512,768]{2,1,0:T(8,128)(2,1)} %dynamic-slice_convert_fusion), channel_id=1, source_target_pairs={{0,1},{1,0},{2,3},{3,2},{4,5},{5,4},{6,7},{7,6},{8,9},{9,8},{10,11... | collective-permute-start | bytes 4718600 | tf_op jit(solution)/shard_map/ppermute | solution.py:482
  276.3 10.0 %copy-start.3 = (bf16[2,1,512,768]{3,2,1,0:T(8,128)(2,1)S(1)}, bf16[2,1,512,768]{3,2,1,0:T(8,128)(2,1)}, u32[]{:S(2)}) copy-start(bf16[2,1,512,768]{3,2,1,0:T(8,128)(2,1)} %param.15) | copy-start | bytes 4718596
  276.3 10.0 %copy-start.16 = (f32[2,512]{1,0:T(2,128)S(1)}, f32[2,512]{1,0:T(2,128)}, u32[]{:S(2)}) copy-start(f32[2,512]{1,0:T(2,128)} %copy-done.15) | copy-start | bytes 12292
  276.3 10.0 %copy-start.19 = (f32[2,512]{1,0:T(2,128)S(1)}, f32[2,512]{1,0:T(2,128)}, u32[]{:S(2)}) copy-start(f32[2,512]{1,0:T(2,128)} %copy-done.18) | copy-start | bytes 12292
  276.3 10.0 %copy-start.21 = (f32[768]{0:T(1024)S(1)}, f32[768]{0:T(1024)}, u32[]{:S(2)}) copy-start(f32[768]{0:T(1024)} %copy-done.20) | copy-start | bytes 9220
  409.8 4.7 %copy-start.8 = (f32[4,48,2304]{2,1,0:T(8,128)S(1)}, f32[4,48,2304]{2,1,0:T(8,128)}, u32[]{:S(2)}) copy-start(f32[4,48,2304]{2,1,0:T(8,128)} %get-tuple-element.40) | copy-start | bytes 5308420
  414.4 1.4 copy-start.13
  414.4 2.7 copy-start.7
  415.8 2.6 copy-start.6

commit v3 on v2

--- a/solution.py
+++ b/solution.py
@@ -12,6 +12,10 @@
 BF16 = jnp.bfloat16
 F32 = jnp.float32
 QB = 256
+TB = 256
+FB = 512
+GELU_A = 0.7978845608028654
+GELU_B = 0.044715
 
 
 def norm_stats(values):
@@ -65,13 +69,17 @@
 
 
 def attention_forward_kernel(factor, size, q_ref, k_ref, v_ref, o_ref, lse_ref):
-    length = q_ref.shape[1]
-    k = k_ref[0]
-    vt = jnp.transpose(v_ref[0])
+    attention_forward_block(factor, size, q_ref.at[0], k_ref.at[0], v_ref.at[0], o_ref.at[0], lse_ref.at[0, 0])
+
+
+def attention_forward_block(factor, size, q_ref, k_ref, v_ref, o_ref, lse_ref):
+    length = q_ref.shape[0]
+    k = k_ref[...]
+    vt = jnp.transpose(v_ref[...])
     for qb in range(length // QB):
         n = (qb + 1) * QB
         rows = pl.ds(qb * QB, QB)
-        q = q_ref[0, rows, :]
+        q = q_ref[rows, :]
         outs = []
         for head in range(2):
             s = causal(dot_nt(k[:n], head_mask(q, head, size)) * factor, qb)
@@ -80,8 +88,8 @@
             total = jnp.sum(p, axis=0, keepdims=True)
             o = dot_nn(vt[head * size : (head + 1) * size, :n], p.astype(BF16))
             outs.append(o * (1.0 / total))
-            lse_ref[0, 0, head : head + 1, rows] = top + jnp.log(total)
-        o_ref[0, rows, :] = jnp.transpose(jnp.concatenate(outs, axis=0)).astype(o_ref.dtype)
+            lse_ref[head : head + 1, rows] = top + jnp.log(total)
+        o_ref[rows, :] = jnp.transpose(jnp.concatenate(outs, axis=0)).astype(o_ref.dtype)
 
 
 def attention_forward(q, k, v, factor, size):
@@ -163,6 +171,143 @@
     )(q, k, v, do, lse)
 
 
+def gelu_parts(b):
+    square = b * b
+    inner = GELU_A * b * (1.0 + GELU_B * square)
+    t = jnp.tanh(inner)
+    rise = 0.5 * (1.0 + t)
+    slope = rise + 0.5 * b * (1.0 - t * t) * (GELU_A * (1.0 + 3.0 * GELU_B * square))
+    return b * rise, slope
+
+
+def middle_kernel(
+    x_ref, mixed_ref, d_ref, wmix_ref, wup_ref, wdown_ref, vec_ref, bup_ref,
+    result_ref, dmid_ref, dmixed_ref, gmix_ref, gup_ref, gdown_ref, gvec_ref, gbup_ref,
+    middle, second, second_t, mixed_t, out_sum, ds_sum, active_t, d_before,
+):
+    step = pl.program_id(0)
+    last = pl.num_programs(0) - 1
+    rows = x_ref.shape[0]
+    chunks = [slice(i, i + TB) for i in range(0, rows, TB)]
+    b_mix, gain, shift, b_down = (vec_ref[i : i + 1, :] for i in range(4))
+
+    @pl.when(step == 0)
+    def _():
+        for at in chunks:
+            mixed = mixed_ref[at]
+            mixed_t[:, at] = jnp.transpose(mixed)
+            mid = x_ref[at].astype(F32) + (dot_nn(mixed, wmix_ref[...]) + b_mix)
+            middle[at] = mid
+            normal, _ = norm_stats(mid)
+            low = (normal * gain + shift).astype(BF16)
+            second[at] = low
+            second_t[:, at] = jnp.transpose(low)
+
+    d_bup = None
+    for at in chunks:
+        act, slope = gelu_parts(dot_nn(second[at], wup_ref[...]) + bup_ref[...])
+        act = act.astype(BF16)
+        active_t[:, at] = jnp.transpose(act)
+        db = (dot_nt(d_ref[at], wdown_ref[...]) * slope).astype(BF16)
+        d_before[at] = db
+        part = jnp.sum(db.astype(F32), axis=0, keepdims=True)
+        d_bup = part if d_bup is None else d_bup + part
+        out = dot_nn(act, wdown_ref[...])
+        ds = dot_nt(db, wup_ref[...])
+
+        @pl.when(step == 0)
+        def _():
+            out_sum[at] = out
+            ds_sum[at] = ds
+
+        @pl.when(step > 0)
+        def _():
+            out_sum[at] += out
+            ds_sum[at] += ds
+
+    gbup_ref[...] = d_bup
+    gdown_ref[...] = dot_nn(active_t[...], d_ref[...]).astype(BF16)
+    gup_ref[...] = dot_nn(second_t[...], d_before[...]).astype(BF16)
+
+    @pl.when(step == last)
+    def _():
+        sums = [None] * 4
+        for at in chunks:
+            mid = middle[at]
+            result_ref[at] = (mid + (out_sum[at] + b_down)).astype(BF16)
+            normal, inverse = norm_stats(mid)
+            ds = ds_sum[at]
+            grad_out = d_ref[at].astype(F32)
+            d_mid = grad_out + norm_back(ds, normal, inverse, gain)
+            dmid_ref[at] = d_mid
+            branch = d_mid.astype(BF16)
+            second[at] = branch
+            dmixed_ref[at] = dot_nt(branch, wmix_ref[...]).astype(BF16)
+            parts = (branch.astype(F32), ds * normal, ds, grad_out)
+            for i, part in enumerate(parts):
+                part = jnp.sum(part, axis=0, keepdims=True)
+                sums[i] = part if sums[i] is None else sums[i] + part
+        for i in range(4):
+            gvec_ref[i : i + 1, :] = sums[i]
+        gmix_ref[...] = dot_nn(mixed_t[...], second[...]).astype(BF16)
+
+
+def middle_block(x, mixed, d_out, w_mix, w_up, w_down, vecs, b_up):
+    rows, width = x.shape
+    ff = w_up.shape[1]
+    whole = lambda shape: pl.BlockSpec(shape, lambda f: (0, 0), pipeline_mode=pl.Buffered(1))
+    out = jax.ShapeDtypeStruct
+    return pl.pallas_call(
+        middle_kernel,
+        grid=(ff // FB,),
+        in_specs=[whole((rows, width))] * 3
+        + [
+            whole((width, width)),
+            pl.BlockSpec((width, FB), lambda f: (0, f)),
+            pl.BlockSpec((FB, width), lambda f: (f, 0)),
+            whole(vecs.shape),
+            pl.BlockSpec((1, FB), lambda f: (0, f)),
+        ],
+        out_specs=[
+            whole((rows, width)),
+            whole((rows, width)),
+            whole((rows, width)),
+            whole((width, width)),
+            pl.BlockSpec((width, FB), lambda f: (0, f)),
+            pl.BlockSpec((FB, width), lambda f: (f, 0)),
+            whole((4, width)),
+            pl.BlockSpec((1, FB), lambda f: (0, f)),
+        ],
+        out_shape=[
+            out((rows, width), BF16),
+            out((rows, width), F32),
+            out((rows, width), BF16),
+            out((width, width), BF16),
+            out((width, ff), BF16),
+            out((ff, width), BF16),
+            out((4, width), F32),
+            out((1, ff), F32),
+        ],
+        scratch_shapes=[
+            pltpu.VMEM((rows, width), F32),
+            pltpu.VMEM((rows, width), BF16),
+            pltpu.VMEM((width, rows), BF16),
+            pltpu.VMEM((width, rows), BF16),
+            pltpu.VMEM((rows, width), F32),
+            pltpu.VMEM((rows, width), F32),
+            pltpu.VMEM((FB, rows), BF16),
+            pltpu.VMEM((rows, FB), BF16),
+        ],
+        compiler_params=pltpu.CompilerParams(vmem_limit_bytes=56 << 20),
+        cost_estimate=pl.CostEstimate(
+            flops=12 * rows * width * ff + 6 * rows * width * width,
+            bytes_accessed=8 * width * ff + 16 * rows * width,
+            transcendentals=rows * ff,
+        ),
+        name="middle_block",
+    )(x, mixed, d_out, w_mix, w_up, w_down, vecs, b_up)
+
+
 MESH = pl.DeviceIdType.MESH
 
 
@@ -215,92 +360,6 @@
 
 def slab(i, half):
     return pl.ds(pl.multiple_of(i * half, 128), half)
-
-
-def gather_kernel(owners, reps, qkv_ref, mix_ref, up_ref, down_ref, small_ref, w_qkv, w_mix, w_up, w_down, w_small, send, recv, kept):
-    z, r, c = position()
-    greet(owners, reps)
-    copies = Copies(send, recv, kept)
-    items = [(mix_ref, w_mix), (up_ref, w_up), (down_ref, w_down)]
-    half = w_qkv.shape[-1] // 3
-    peers_z = [{"fsdp": lax.rem(z + j, owners)} for j in range(1, owners)]
-    origins = [lax.rem(z - j + owners, owners) for j in range(1, owners)]
-    peers_r = [{"rep": r ^ k} for k in range(1, reps)]
-
-    small = [copies.remote(small_ref, w_small.at[z], to) for to in peers_z]
-    first = [
-        [
-            copies.remote(qkv_ref.at[r, :, slab(2 * i + c, half)], w_qkv.at[z, r, :, slab(i, half)], to)
-            for i in range(3)
-        ]
-        for to in peers_z
-    ]
-    rest = [[copies.remote(shard.at[c, r], whole.at[z, c, r], to) for to in peers_z] for shard, whole in items]
-    copies.keep(small_ref, w_small.at[z])
-    for i in range(3):
-        copies.keep(qkv_ref.at[:, :, slab(2 * i + c, half)], w_qkv.at[z, :, :, slab(i, half)])
-    for shard, whole in items:
-        copies.keep(shard, whole.at[z])
-
-    spread = []
-    for arrived, origin in zip(first, origins):
-        for copy in arrived:
-            copy.wait_recv()
-        piece = w_qkv.at[origin, r]
-        spread += [copies.remote(piece, piece, to) for to in peers_r]
-    spread_rest = []
-    for (shard, whole), arrived in zip(items, rest):
-        for copy, origin in zip(arrived, origins):
-            copy.wait_recv()
-            piece = whole.at[origin, c, r]
-            spread_rest.append((whole.at[origin, c], [copies.remote(piece, piece, to) for to in peers_r]))
-    last = []
-    for side, arrived in spread_rest:
-        for copy in arrived:
-            copy.wait_recv()
-        last.append(copies.remote(side, side, {"ctx": 1 - c}))
-    for copy in small + spread + last:
-        copy.wait_recv()
-    copies.close()
-    for copy in copies.kept:
-        copy.wait()
-
-
-def gather_weights(owners, reps, weight_qkv, weight_mix, weight_up, weight_down, small):
-    own, wide = weight_qkv.shape
-
-    def cut(shard):
-        return shard.reshape(2, reps, shard.shape[0] // (2 * reps), shard.shape[1])
-
-    ins = (
-        weight_qkv.reshape(reps, own // reps, wide),
-        cut(weight_mix),
-        cut(weight_up),
-        cut(weight_down),
-        small,
-    )
-    shapes = [(owners, reps, own // reps, wide // 2)] + [(owners,) + x.shape for x in ins[1:]]
-    remotes = (owners - 1) * (4 + 3 + 4 * (reps - 1) + 3)
-    whole = pl.pallas_call(
-        partial(gather_kernel, owners, reps),
-        in_specs=[pl.BlockSpec(memory_space=pl.ANY)] * 5,
-        out_specs=[pl.BlockSpec(memory_space=pl.ANY)] * 5,
-        out_shape=[jax.ShapeDtypeStruct(s, BF16) for s in shapes],
-        scratch_shapes=[
-            pltpu.SemaphoreType.DMA((remotes,)),
-            pltpu.SemaphoreType.DMA((remotes,)),
-            pltpu.SemaphoreType.DMA((7,)),
-        ],
-        compiler_params=pltpu.CompilerParams(collective_id=1, has_side_effects=True),
-        name="gather_weights",
-    )(*ins)
-    return (
-        whole[0].reshape(owners * own, wide // 2),
-        whole[1].reshape(owners * own, -1),
-        whole[2].reshape(owners * own, -1),
-        whole[3].reshape(owners * weight_down.shape[0], -1),
-        whole[4],
-    )
 
 
 def add_blocks(out, parts, dtype):
@@ -450,6 +509,308 @@
     )
 
 
+class Plan:
+    def __init__(self, send, recv):
+        self.send, self.recv = send, recv
+        self.made = {}
+
+    def add(self, name, src, dst, peer):
+        self.made[name] = (len(self.made), src, dst, peer)
+
+    def copy(self, name):
+        slot, src, dst, peer = self.made[name]
+        return pltpu.make_async_remote_copy(
+            src_ref=src(),
+            dst_ref=dst(),
+            send_sem=self.send.at[slot],
+            recv_sem=self.recv.at[slot],
+            device_id=peer,
+            device_id_type=MESH,
+        )
+
+    def start(self, *names):
+        for name in names:
+            self.copy(name).start()
+
+    def arrive(self, *names):
+        for name in names:
+            self.copy(name).wait_recv()
+
+    def close(self):
+        for name in self.made:
+            self.copy(name).wait_send()
+
+
+def spread_plan(plan, tag, owners, reps, z, r, c, src, dst, halves, core=None):
+    for j in range(1, owners):
+        origin = lax.rem(z - j + owners, owners)
+        plan.add((tag, "z", j), src, lambda: dst(z, r), {"fsdp": lax.rem(z + j, owners)})
+        here = partial(dst, origin, r)
+        plan.add((tag, "x", j), here, here, {"rep": r ^ 1})
+        plan.add((tag, "y", j), here, here, {"rep": r ^ 2})
+        by_y = lambda origin=origin: halves(dst(origin, r ^ 2))[0]
+        by_x = lambda origin=origin: halves(dst(origin, r ^ 1))[1]
+        plan.add((tag, "xx", j), by_y, by_y, {"rep": r ^ 1})
+        plan.add((tag, "yy", j), by_x, by_x, {"rep": r ^ 2})
+        if core is not None:
+            side = partial(core, origin)
+            plan.add((tag, "c", j), side, side, {"ctx": 1 - c})
+
+
+def spread_step(plan, tag, owners, stage):
+    for j in range(1, owners):
+        if stage == 0:
+            plan.start((tag, "z", j))
+        elif stage == 1:
+            plan.arrive((tag, "z", j))
+            plan.start((tag, "x", j), (tag, "y", j))
+        elif stage == 2:
+            plan.arrive((tag, "y", j))
+            plan.start((tag, "xx", j))
+            plan.arrive((tag, "x", j))
+            plan.start((tag, "yy", j))
+        elif stage == 3:
+            plan.arrive((tag, "xx", j), (tag, "yy", j))
+            if (tag, "c", j) in plan.made:
+                plan.start((tag, "c", j))
+        else:
+            plan.arrive((tag, "c", j))
+
+
+def forward_kernel(owners, reps, pairs, factor, size,
+                   x_ref, qkv_ref, mix_ref, up_ref, down_ref, small_ref,
+                   mixed, qkv_out, first_t_out, w_qkv_out, w_mix, w_up, w_down, vec_ref, lse_ref,
+                   first, first_t, w_qkv, qkv, heads, small, send, recv, kept):
+    step = pl.program_id(0)
+    last = pl.num_programs(0) - 1
+    z, r, c = position()
+    mbs, rows, width = x_ref.shape
+    half = width // 2
+    lanes = 2 * size
+    plan = Plan(send, recv)
+    own_rows = pl.ds(pl.multiple_of(c * rows, rows), rows)
+    their_rows = pl.ds(pl.multiple_of((1 - c) * rows, rows), rows)
+
+    for j in range(1, owners):
+        plan.add(("small", j), lambda: small_ref, lambda: small.at[z], {"fsdp": lax.rem(z + j, owners)})
+    for m in range(mbs):
+        plan.add(("first", m), lambda m=m: first.at[m, own_rows], lambda m=m: first.at[m, own_rows], {"ctx": 1 - c})
+    for j in range(1, owners):
+        for i in range(3):
+            plan.add(
+                ("qkv", "z", i, j),
+                lambda i=i: qkv_ref.at[r, :, slab(2 * i + c, half)],
+                lambda i=i: w_qkv.at[z, r, :, slab(i, half)],
+                {"fsdp": lax.rem(z + j, owners)},
+            )
+    cut = w_qkv.shape[3] // 256 * 128
+    spread_plan(
+        plan, "qkv", owners, reps, z, r, c, None, lambda o, p: w_qkv.at[o, p],
+        lambda ref: (ref.at[:, pl.ds(0, cut)], ref.at[:, pl.ds(cut, 3 * half - cut)]),
+    )
+    for j in range(1, owners):
+        del plan.made[("qkv", "z", j)]
+    tags = []
+
+    def chunk(tag, shard, whole, by_rows, parts):
+        n = shard.shape[2 if by_rows else 3] // parts
+
+        def part(ref, k):
+            span = pl.ds(k * n, n)
+            return ref.at[span] if by_rows else ref.at[:, span]
+
+        def halves(ref):
+            middle = ref.shape[1] // 2
+            return ref.at[:, pl.ds(0, middle)], ref.at[:, pl.ds(middle, middle)]
+
+        for k in range(parts):
+            tags.append((tag, k))
+            spread_plan(
+                plan, (tag, k), owners, reps, z, r, c,
+                lambda k=k: part(shard.at[c, r], k),
+                lambda o, p, k=k: part(whole.at[o, c, p], k),
+                halves,
+                lambda o, k=k: (whole.at[o, c, :, pl.ds(k * n, n)] if by_rows else whole.at[o, c, :, :, pl.ds(k * n, n)]),
+            )
+
+    chunk("mix", mix_ref, w_mix, False, 1)
+    chunk("up", up_ref, w_up, False, 2)
+    chunk("down", down_ref, w_down, True, 2)
+    order = [tags[0], tags[1], tags[3], tags[2], tags[4]]
+    plan.made = {name: (i,) + rest[1:] for i, (name, rest) in enumerate(plan.made.items())}
+
+    def keep(i):
+        copies = [(small_ref, small.at[z])]
+        copies += [(qkv_ref.at[:, :, slab(2 * i + c, half)], w_qkv.at[z, :, :, slab(i, half)]) for i in range(3)]
+        copies += [(mix_ref, w_mix.at[z]), (up_ref, w_up.at[z]), (down_ref, w_down.at[z])]
+        copies += [(w_qkv, w_qkv_out), (first_t, first_t_out), (qkv, qkv_out)]
+        return pltpu.make_async_copy(*copies[i], kept.at[i])
+
+    def mixed_place(step):
+        m, p = lax.div(step, pairs), lax.rem(step, pairs)
+        return mixed.at[m, :, slab(c * pairs + p, lanes)]
+
+    def mixed_sends(k, slot):
+        return pltpu.make_async_remote_copy(
+            src_ref=heads.at[k, their_rows],
+            dst_ref=mixed_place(k),
+            send_sem=send.at[slot],
+            recv_sem=recv.at[slot],
+            device_id={"ctx": 1 - c},
+            device_id_type=MESH,
+        )
+
+    base = len(plan.made)
+
+    @pl.when(step == 0)
+    def _():
+        greet(owners, reps)
+        for i in range(7):
+            keep(i).start()
+        plan.start(*[("small", j) for j in range(1, owners)])
+        for j in range(1, owners):
+            plan.start(*[("qkv", "z", i, j) for i in range(3)])
+        keep(0).wait()
+        plan.arrive(*[("small", j) for j in range(1, owners)])
+        vec_ref[...] = jnp.transpose(small[...].reshape(-1, small.shape[-1]))[:16]
+        gain, shift = vec_ref[3:4, :], vec_ref[4:5, :]
+        for m in range(mbs):
+            for at in range(0, rows, TB):
+                normal, _ = norm_stats(x_ref[m, at : at + TB].astype(F32))
+                place = pl.ds(pl.multiple_of(c * rows + at, TB), TB)
+                first[m, place] = (normal * gain + shift).astype(BF16)
+            plan.start(("first", m))
+        for j in range(1, owners):
+            plan.arrive(*[("qkv", "z", i, j) for i in range(3)])
+            plan.start(("qkv", "x", j), ("qkv", "y", j))
+        for tag in order:
+            spread_step(plan, tag, owners, 0)
+        plan.arrive(*[("first", m) for m in range(mbs)])
+        for m in range(mbs):
+            for at in range(0, 2 * rows, TB):
+                first_t[:, m * 2 * rows + at : m * 2 * rows + at + TB] = jnp.transpose(first[m, at : at + TB])
+        keep(8).start()
+        spread_step(plan, "qkv", owners, 2)
+        spread_step(plan, "qkv", owners, 3)
+        for i in range(1, 4):
+            keep(i).wait()
+        keep(7).start()
+        weight = w_qkv[...].reshape(-1, w_qkv.shape[-1])
+        b_query = vec_ref[0:1, slab(c, half)]
+        b_value = vec_ref[1:2, slab(c, half)]
+        bias = jnp.concatenate([b_query, jnp.zeros_like(b_query), b_value], axis=1)
+
+        def project_rows(i, _):
+            m, at = lax.div(i, 2 * rows // TB), lax.rem(i, 2 * rows // TB)
+            place = pl.ds(pl.multiple_of(at * TB, TB), TB)
+            joined = (dot_nn(first[m, place], weight) + bias).astype(BF16)
+            for s in range(3 * pairs):
+                qkv[m, s, place] = joined[:, s * lanes : (s + 1) * lanes]
+            return 0
+
+        lax.fori_loop(0, mbs * 2 * rows // TB, project_rows, 0)
+        keep(9).start()
+
+    moves = {
+        1: [(0, 1)],
+        2: [(0, 2), (1, 1)],
+        3: [(0, 3), (1, 2), (2, 1)],
+        4: [(0, 4), (1, 3), (2, 2), (3, 1)],
+        5: [(1, 4), (2, 3), (3, 2), (4, 1)],
+        6: [(2, 4), (3, 3), (4, 2)],
+    }
+    for k, some in moves.items():
+
+        @pl.when(step == k)
+        def _():
+            for t, stage in some:
+                spread_step(plan, order[t], owners, stage)
+
+    @pl.when(step > 0)
+    def _():
+        k = step - 1
+        m, p = lax.div(k, pairs), lax.rem(k, pairs)
+        attention_forward_block(
+            factor, size, qkv.at[m, p], qkv.at[m, pairs + p], qkv.at[m, 2 * pairs + p], heads.at[k], lse_ref.at[m, p]
+        )
+        mixed_sends(k, base + k).start()
+        pltpu.make_async_copy(heads.at[k, own_rows], mixed_place(k), kept.at[10 + k]).start()
+
+    @pl.when(step == last)
+    def _():
+        spread_step(plan, order[3], owners, 4)
+        spread_step(plan, order[4], owners, 3)
+        spread_step(plan, order[4], owners, 4)
+        for k in range(mbs * pairs):
+            mixed_sends(k, base + k).wait()
+            pltpu.make_async_copy(heads.at[k, own_rows], mixed_place(k), kept.at[10 + k]).wait()
+        plan.close()
+        for i in range(4, 10):
+            keep(i).wait()
+
+
+def forward_block(x, weight_qkv, weight_mix, weight_up, weight_down, small, owners, reps, factor, size):
+    own, wide = weight_qkv.shape
+    mbs, rows, width = x.shape
+    lanes = 2 * size
+    pairs = width // 2 // lanes
+
+    def cut(shard):
+        return shard.reshape(2, reps, shard.shape[0] // (2 * reps), shard.shape[1])
+
+    shards = (weight_qkv.reshape(reps, own // reps, wide), cut(weight_mix), cut(weight_up), cut(weight_down), small)
+    shape = jax.ShapeDtypeStruct
+    w_shape = (owners, reps, own // reps, wide // 2)
+    qkv_shape = (mbs, 3 * pairs, 2 * rows, lanes)
+    anywhere = pl.BlockSpec(memory_space=pl.ANY)
+    whole = lambda s: pl.BlockSpec(s, lambda i: (0,) * len(s), pipeline_mode=pl.Buffered(1))
+    remotes = 3 + mbs + 9 + 12 + 5 * 18 + mbs * pairs
+    area = mbs * pairs * 2 * rows * (2 * rows + QB)
+    mixed, qkv, first_t, w_qkv, w_mix, w_up, w_down, vecs, lse = pl.pallas_call(
+        partial(forward_kernel, owners, reps, pairs, factor, size),
+        grid=(1 + mbs * pairs,),
+        in_specs=[whole(x.shape)] + [anywhere] * 5,
+        out_specs=[anywhere] * 7 + [whole((16, width)), whole((mbs, pairs, 8, 2 * rows))],
+        out_shape=[
+            shape((mbs, rows, width), BF16),
+            shape(qkv_shape, BF16),
+            shape((width, mbs * 2 * rows), BF16),
+            shape(w_shape, BF16),
+            shape((owners,) + shards[1].shape, BF16),
+            shape((owners,) + shards[2].shape, BF16),
+            shape((owners,) + shards[3].shape, BF16),
+            shape((16, width), F32),
+            shape((mbs, pairs, 8, 2 * rows), F32),
+        ],
+        scratch_shapes=[
+            pltpu.VMEM((mbs, 2 * rows, width), BF16),
+            pltpu.VMEM((width, mbs * 2 * rows), BF16),
+            pltpu.VMEM(w_shape, BF16),
+            pltpu.VMEM(qkv_shape, BF16),
+            pltpu.VMEM((mbs * pairs, 2 * rows, lanes), BF16),
+            pltpu.VMEM((owners,) + small.shape, F32),
+            pltpu.SemaphoreType.DMA((remotes,)),
+            pltpu.SemaphoreType.DMA((remotes,)),
+            pltpu.SemaphoreType.DMA((10 + mbs * pairs,)),
+        ],
+        compiler_params=pltpu.CompilerParams(
+            collective_id=1, has_side_effects=True, vmem_limit_bytes=56 << 20
+        ),
+        name="forward_block",
+    )(x, *shards)
+    return (
+        mixed,
+        qkv,
+        first_t,
+        w_qkv.reshape(owners * own, -1),
+        w_mix.reshape(owners * own, -1),
+        w_up.reshape(owners * own, -1),
+        w_down.reshape(owners * weight_down.shape[0], -1),
+        vecs,
+        lse,
+    )
+
+
 def local(
     inputs,
     weight_qkv,
@@ -477,6 +838,7 @@
     ctx = lax.axis_index("ctx")
     rep = lax.axis_index("rep")
     own = weight_qkv.shape[0]
+    direct = own % (16 * reps) == 0 and owners == 4 and reps == 4
 
     def swap(x):
         return lax.ppermute(x, "ctx", [(0, 1), (1, 0)])
@@ -492,14 +854,23 @@
         return lax.dynamic_slice_in_dim(x, which * half, half, axis)
 
     direct = own % (16 * reps) == 0 and owners == 4 and reps == 4
-    rows8 = jnp.stack(
-        [bias_query, bias_value, bias_mix, gain_attn, shift_attn, gain_mlp, shift_mlp, bias_down]
-    )
-    small = jnp.concatenate([rows8, bias_up.reshape(-1, own), jnp.zeros((4, own), BF16)], axis=0)
+    vectors = [bias_query, bias_value, bias_mix, gain_attn, shift_attn, gain_mlp, shift_mlp, bias_down]
+    small = jnp.stack(vectors + [v for v in bias_up.reshape(-1, own)], axis=1).astype(F32)
+    tokens = inputs[:, 0].astype(F32)
     if direct:
-        w_qkv, w_mix, w_up, w_down, small = gather_weights(
-            owners, reps, weight_qkv, weight_mix, weight_up, weight_down, small
+        mixed, qkv, first_t, w_qkv, w_mix, w_up, w_down, vecs, lse = forward_block(
+            inputs[:, 0],
+            weight_qkv,
+            weight_mix,
+            weight_up,
+            weight_down,
+            jnp.pad(small, ((0, 0), (0, 128 - small.shape[1]))),
+            owners,
+            reps,
+            factor,
+            size,
         )
+        vecs = vecs[:12]
     else:
         part = own // reps
         mine = lax.dynamic_slice_in_dim(weight_qkv, rep * part, part, 0)
@@ -514,20 +885,19 @@
         w_mix = gather(weight_mix)
         w_up = gather(weight_up)
         w_down = gather(weight_down)
-        small = lax.all_gather(small, "fsdp")
-    small = small.astype(F32)
-    b_query, b_value, b_mix, g_attn, s_attn, g_mlp, s_mlp, b_down = (small[:, i].reshape(-1) for i in range(8))
-    b_up = small[:, 8:-4].reshape(-1)
-
-    tokens = inputs[:, 0].astype(F32)
+        vecs = lax.all_gather(small, "fsdp", axis=0, tiled=True).T
+    b_query, b_value, b_mix, g_attn, s_attn, g_mlp, s_mlp, b_down = (vecs[i] for i in range(8))
+    b_up = vecs[8:].reshape(-1, owners, own).swapaxes(0, 1).reshape(-1)
+
     normal_one, inverse_one = norm_stats(tokens)
-    first_own = (normal_one * g_attn + s_attn).astype(BF16)
-    first = order(first_own, swap(first_own), 1)
-    joined = project(first, w_qkv)
-    query = (joined[..., :half] + columns(b_query, 0, ctx)).astype(BF16)
-    key = joined[..., half : 2 * half].astype(BF16)
-    value = (joined[..., 2 * half :] + columns(b_value, 0, ctx)).astype(BF16)
-    mixed_heads, lse = attention_forward(query, key, value, factor, size)
+    if not direct:
+        first_own = (normal_one * g_attn + s_attn).astype(BF16)
+        first = order(first_own, swap(first_own), 1)
+        joined = project(first, w_qkv)
+        query = (joined[..., :half] + columns(b_query, 0, ctx)).astype(BF16)
+        key = joined[..., half : 2 * half].astype(BF16)
+        value = (joined[..., 2 * half :] + columns(b_value, 0, ctx)).astype(BF16)
+        mixed_heads, lse = attention_forward(query, key, value, factor, size)
 
     def my_rows(x):
         return lax.dynamic_slice_in_dim(x, ctx * rows, rows, 1)
@@ -535,32 +905,28 @@
     def their_rows(x):
         return lax.dynamic_slice_in_dim(x, (1 - ctx) * rows, rows, 1)
 
-    mixed = order(my_rows(mixed_heads), swap(their_rows(mixed_heads)), 2)
-    middle = tokens + project(mixed, w_mix) + b_mix
-    normal_two, inverse_two = norm_stats(middle)
-    second = (normal_two * g_mlp + s_mlp).astype(BF16)
-    before = project(second, w_up) + b_up
-    active, gelu_back = jax.vjp(partial(jax.nn.gelu, approximate=True), before)
-    active = active.astype(BF16)
-    result = (middle + project(active, w_down) + b_down).astype(BF16)
-
-    d_down = cotangent[:, 0]
-    grad_out = d_down.astype(F32)
-    g_wdown = outer_sum(active, d_down)
-    g_bdown = jnp.sum(grad_out, axis=(0, 1))
-    d_before_f = gelu_back(project_back(d_down, w_down))[0]
-    d_before = d_before_f.astype(BF16)
-    g_wup = outer_sum(second, d_before)
-    g_bup = jnp.sum(d_before.astype(F32), axis=(0, 1))
-    d_second = project_back(d_before, w_up)
-    g_gmlp = jnp.sum(d_second * normal_two, axis=(0, 1))
-    g_smlp = jnp.sum(d_second, axis=(0, 1))
-    d_middle = grad_out + norm_back(d_second, normal_two, inverse_two, g_mlp)
-    d_branch = d_middle.astype(BF16)
-    g_wmix = outer_sum(mixed, d_branch)
-    g_bmix = jnp.sum(d_branch.astype(F32), axis=(0, 1))
-    d_mixed = project_back(d_branch, w_mix).astype(BF16)
+    if not direct:
+        mixed = order(my_rows(mixed_heads), swap(their_rows(mixed_heads)), 2)
+    flat = (-1, width)
+    result, d_middle, d_mixed, g_wmix, g_wup, g_wdown, g_vecs, g_bup = middle_block(
+        inputs.reshape(flat),
+        mixed.reshape(flat),
+        cotangent.reshape(flat),
+        w_mix,
+        w_up,
+        w_down,
+        jnp.stack([b_mix, g_mlp, s_mlp, b_down]),
+        b_up.reshape(1, -1),
+    )
+    g_bmix, g_gmlp, g_smlp, g_bdown = (g_vecs[i] for i in range(4))
+    d_mixed = d_mixed.reshape(tokens.shape)
+    d_middle = d_middle.reshape(tokens.shape)
     d_heads = order(columns(d_mixed, 2, ctx), swap(columns(d_mixed, 2, 1 - ctx)), 1)
+    if direct:
+        query, key, value = (
+            qkv[:, i * n : (i + 1) * n].swapaxes(1, 2).reshape(d_heads.shape) for n in [qkv.shape[1] // 3] for i in range(3)
+        )
+        first = first_t.T.reshape(d_heads.shape[:2] + (width,))
     d_query, d_key, d_value = attention_backward(query, key, value, d_heads, lse, factor, size)
     d_joined = jnp.concatenate([d_query, d_key, d_value], axis=-1)
     g_wqkv = outer_sum(first, d_joined)
@@ -610,7 +976,7 @@
     o_bq, o_bv, o_bmix, o_ga, o_sa, o_gm, o_sm, o_bd = (summed[i] for i in range(8))
     o_bup = summed[8:-4].reshape(-1)
     return (
-        result[:, None],
+        result.reshape(inputs.shape),
         d_tokens[:, None],
         o_wqkv,
         o_bq,

time: 427 us -> 372 us (0.87)
  matrix products: 95.8 us -> 13.1 us
  local copies, waits for them, and re-layouts: 23.1 us -> 44.6 us
  Pallas kernels: 273 us -> 292 us
  other arithmetic: 20.9 us -> 13.7 us
  waiting for transfers between devices: 4.39 us -> 0.01 us
    dot_general x4 -> x0, matrix products: 30.2 us -> none  [project(): return jnp.einsum('sri,ij->srj', left, weight, preferred_element_type=F32)]
    dot_general x4 -> x1, matrix products: 35.3 us -> 8.86 us  [outer_sum(): return jnp.einsum('sri,srj->ij', left, right, preferred_element_type=F32)]
    dot_general x4 -> x1, matrix products: 30.3 us -> 4.28 us  [project_back(): jnp.einsum('srj,ij->sri', grad_rows, weight, preferred_element_type=F32)]
    pallas_call x2, Pallas kernels: 126 us -> 146 us  [the longest x1 90.1 us: forward_block(): pl.pallas_call(partial(forward_kernel, owners, reps, pairs, factor, size)...]
    transpose x0 -> x4, local copies, waits for them, and re-layouts: none -> 9.57 us  [local(): qkv[:, i * n:(i + 1) * n].swapaxes(1, 2).reshape(d_heads.shape)]
    reshape x1 -> x5, local copies, waits for them, and re-layouts: 0.77 us -> 7.92 us  [the longest x3 7.82 us: local(): qkv[:, i * n:(i + 1) * n].swapaxes(1, 2).reshape(d_heads.shape)]
    ppermute x4 -> x2, waiting for transfers between devices: 4.39 us -> 0.01 us  [swap(): return lax.ppermute(x, 'ctx', [(0, 1), (1, 0)])]
  transfers between devices with their start and end apart: 4 -> 2, of which waited for: 2 -> 0; matrix products, arithmetic and copies ran while one was open for 6% -> 8% of each run, Pallas kernels for 0% -> 0%
where the time goes in v3:
time: 372 us; the launch traced here: 366 us
  Pallas kernels  292 us (78%)
  local copies, waits for them, and re-layouts  44.6 us (12%)
  other arithmetic  13.7 us (4%)
  matrix products  13.1 us (4%)
    pallas_call x1, Pallas kernels, reduce_grads(): pl.pallas_call(partial(reduce_kernel, owners, reps), in_specs=[pl.BlockSp...  114 us
    pallas_call x1, Pallas kernels, forward_block(): pl.pallas_call(partial(forward_kernel, owners, reps, pairs, factor, size)...  90.1 us
    pallas_call x1, Pallas kernels, middle_block(): pl.pallas_call(middle_kernel, grid=(ff // FB,), in_specs=[whole((rows, wi...  55.9 us
    pallas_call x1, Pallas kernels, attention_backward(): pl.pallas_call(partial(attention_backward_kernel, factor, size), grid=(mb...  32 us
    transpose x4, local copies, waits for them, and re-layouts, local(): qkv[:, i * n:(i + 1) * n].swapaxes(1, 2).reshape(d_heads.shape)  9.57 us
    dot_general x1, matrix products, outer_sum(): return jnp.einsum('sri,srj->ij', left, right, preferred_element_type=F32)  8.86 us
    reshape x3, local copies, waits for them, and re-layouts, local(): qkv[:, i * n:(i + 1) * n].swapaxes(1, 2).reshape(d_heads.shape)  7.82 us
  transfers between devices with their start and end apart: 2, of which 0 were waited for; matrix products, arithmetic and copies ran while one was open for 8% of the time, Pallas kernels for 0%

profile of v3, /device:TPU:1, one launch (start us, length us, event | category | flops | bytes accessed | tf_op | source)
XLA Modules:
  0.0 365.7 jit_solution(17604931550443962510)
XLA Ops:
  0.6 0.9 fusion.16
  1.6 0.7 stack.30
  2.2 0.7 stack.31
  2.9 0.7 stack.32
  3.6 0.7 stack.33
  4.2 0.7 stack.34
  4.9 0.7 stack.35
  5.5 0.7 stack.36
  6.2 0.7 stack.37
  7.0 0.7 pad_convert_fusion.small_ref
  7.7 90.1 %forward_block.1 = (bf16[2,512,768]{2,1,0:T(8,128)(2,1)}, bf16[2,9,1024,128]{3,2,1,0:T(8,128)(2,1)}, bf16[768,2048]{1,0:T(8,128)(2,1)}, bf16[4,4,48,1152]{3,2,1,...) custom-call(bf16[2,512,768]{2,1,0:T(8,128)(2,1)} %bitcast.68, ...), custom_call_target="tpu_custom_call" | custom-call | tf_op jit(solution)/shard_map/forward_block/pallas_call | solution.py:769
  97.8 0.8 slice_reduce_fusion.4
  98.6 0.7 slice.75
  99.4 0.7 slice.76
  100.2 0.7 reshape_reshape.3.bup_ref
  100.9 0.6 pad_maximum_fusion.vec_ref
  101.5 55.9 %middle_block.1 = (bf16[1024,768]{1,0:T(8,128)(2,1)}, f32[1024,768]{1,0:T(8,128)}, bf16[1024,768]{1,0:T(8,128)(2,1)}, bf16[768,768]{1,0:T(8,128)(2,1)}, bf16[768...) custom-call(bf16[1024,768]{1,0:T(8,128)(2,1)} %bitcast.69, ...), custom_call_target="tpu_custom_call" | custom-call | flops 32614907904 | bytes 31457280 | tf_op jit(solution)/shard_map/middle_block/pallas_call | solution.py:260
  157.4 2.7 constant_dynamic-slice_fusion.1
  160.1 1.0 collective-permute-start
  161.1 3.9 %slice_bitcast_fusion = (bf16[2,1024,3,128]{3,1,2,0:T(8,128)(2,1)S(1)}, bf16[2,1024,3,128]{3,1,2,0:T(8,128)(2,1)S(1)}, bf16[2,1024,3,128]{3,1,2,0:T(8,128)(2,1)}) fusion(bf16[2,9,1024,128]{3,2,1,0:T(8,128)(2,1)} %get-tuple-element.47), kind=kLoop, calls=%fused_computation.24 | loop fusion | bytes 9437184 | tf_op jit(solution)/shard_map/transpose | solution.py:927
  164.9 2.6 copy.61
  167.5 2.6 copy.64.q_ref
  170.1 1.6 copy.62
  171.6 2.6 copy.65.k_ref
  174.2 1.6 copy.63
  175.8 2.7 copy.66.v_ref
  178.8 0.5 broadcast.47
  179.3 0.7 reduce.13
  180.4 2.9 maximum_select_fusion.do_ref
  183.4 32.0 %attention_backward.1 = (bf16[2,1024,384]{2,1,0:T(8,128)(2,1)S(1)}, bf16[2,1024,384]{2,1,0:T(8,128)(2,1)S(1)}, bf16[2,1024,384]{2,1,0:T(8,128)(2,1)S(1)}) custom-call(bf16[2,1024,384]{2,1,0:T(8,128)(2,1)} %copy.64.q_ref, bf16[2,1024,384]{2,1,0:T(8,128)(2,1)} %copy.65.k_ref, bf16[2,1024,384]{2,1,0:T(8,128)(2,1)} %copy.66.v_ref, ...), custom_call_target="tpu_custom_call" | custom-call | flops 20132659200 | bytes 11010048 | tf_op jit(solution)/shard_map/attention_backward/pallas_call | solution.py:159
  216.2 0.8 copy-done.12
  217.0 4.3 %fusion.17 = f32[2,1024,768]{2,1,0:T(8,128)S(1)} fusion(bf16[2,1024,1152]{2,1,0:T(8,128)(2,1)S(1)} %constant_dynamic-update-slice_fusion, bf16[768,1152,1]{1,0,2:T(8,128)(2,1)S(1)} %bitcast.99), kind=kOutput, calls=%fused_computation.46 | convolution fusion | flops 3623878656 | bytes 12779520 | tf_op jit(solution)/shard_map/srj,ij->sri/dot_general | solution.py:45
  221.3 1.5 dynamic-slice_convert_fusion
  222.8 0.6 fusion.12
  223.4 0.5 convert_reduce_fusion.1
  223.9 0.6 copy-done.2
  225.0 8.9 %fusion.5 = bf16[768,1152]{1,0:T(8,128)(2,1)} fusion(bf16[2,1024,1152]{2,1,0:T(8,128)(2,1)} %copy-done.9, bf16[96,2,8,1024]{3,2,1,0:T(8,128)(2,1)} %bitcast.98), kind=kOutput, calls=%fused_computation.8 | convolution fusion | flops 3624763392 | bytes 9633792 | tf_op jit(solution)/shard_map/sri,srj->ij/dot_general | solution.py:37
  233.8 2.8 fusion.11
  236.9 1.3 concatenate.15.refs_4_
  238.2 114.0 %reduce_grads.1 = (f32[2,4,96,768]{3,2,1,0:T(8,128)}, f32[2,4,24,3072]{3,2,1,0:T(8,128)}, f32[2,4,24,768]{3,2,1,0:T(8,128)}, f32[4,48,2304]{2,1,0:T(8,128)}, f32[16,192]{1,0:T(8,128)}) custom-call(bf16[4,2,4,96,768]{4,3,2,1,0:T(8,128)(2,1)} %bitcast.74, bf16[4,2,4,24,3072]{4,3,2,1,0:T(8,128)(2,1)} %bitcast.73, bf16[4,2,4,24,768]{4,3,2,1,0:T(8,128)(2,1)} %bitcast.81, ...), custom_call_target="tpu_custom_call" | custom-call | tf_op jit(solution)/shard_map/reduce_grads/pallas_call | solution.py:494
  352.1 1.6 fusion.15
  353.7 0.7 slice.92
  354.4 0.7 reshape.174
  355.1 4.6 %fusion.10 = f32[2,1,512,768]{3,2,1,0:T(8,128)} fusion(f32[2,512,768]{2,1,0:T(8,128)} %bitcast.75, f32[2,512,768]{2,1,0:T(8,128)} %get-tuple-element.118, f32[2,512]{1,0:T(2,128)S(1)} %get-tuple-element.140, f32[2,512]{1,0:T(2,128)S(1)} %get-tuple-element.141, f32[768]{0:T(1024)S(1)} %get-tuple-element.124, f32[2,512]{1,0:T(2,128)S(1)} %add_rsqrt_fusion, ...), kind=kLoop, calls=%fused_computation.13 | loop fusion | flops 7077888 | bytes 11029504
  359.8 1.2 copy.85
  361.2 0.8 copy.86
  362.4 1.4 copy.87
  363.8 1.4 copy.88
  (57 shorter events, 3.2 us)
Async XLA Ops:
  160.1 20.3 %collective-permute-start = (bf16[2,512,384]{2,1,0:T(8,128)(2,1)}, bf16[2,512,384]{2,1,0:T(8,128)(2,1)}, u32[]{:S(2)}, u32[]{:S(2)}) collective-permute-start(bf16[2,512,384]{2,1,0:T(8,128)(2,1)} %get-tuple-element.123), channel_id=1, source_target_pairs={{0,1},{1,0},{2,3},{3,2},{4,5},{5,4},{6,7},{7,6},{8,9},{9,8},{10,11... | collective-permute-start | bytes 2359304 | tf_op jit(solution)/shard_map/ppermute | solution.py:844
  174.2 4.3 %copy-start.10 = (f32[4,768]{1,0:T(4,128)S(1)}, f32[4,768]{1,0:T(4,128)}, u32[]{:S(2)}) copy-start(f32[4,768]{1,0:T(4,128)} %get-tuple-element.58) | copy-start | bytes 36868
  174.2 5.1 %copy-start.11 = (f32[1,3072]{1,0:T(1,128)S(1)}, f32[1,3072]{1,0:T(1,128)}, u32[]{:S(2)}) copy-start(f32[1,3072]{1,0:T(1,128)} %get-tuple-element.59) | copy-start | bytes 36868
  174.2 5.9 %copy-start.1 = (bf16[2,1,512,768]{3,2,1,0:T(8,128)(2,1)S(1)}, bf16[2,1,512,768]{3,2,1,0:T(8,128)(2,1)}, u32[]{:S(2)}) copy-start(bf16[2,1,512,768]{3,2,1,0:T(8,128)(2,1)} %param.15) | copy-start | bytes 4718596
  175.8 4.6 %copy-start.4 = (bf16[2,512,384]{2,1,0:T(8,128)(2,1)S(1)}, bf16[2,512,384]{2,1,0:T(8,128)(2,1)}, u32[]{:S(2)}) copy-start(bf16[2,512,384]{2,1,0:T(8,128)(2,1)} %get-tuple-element.122) | copy-start | bytes 2359300
  178.5 4.9 %copy-start = (f32[2,3,8,1024]{3,2,1,0:T(8,128)S(1)}, f32[2,3,8,1024]{3,2,1,0:T(8,128)}, u32[]{:S(2)}) copy-start(f32[2,3,8,1024]{3,2,1,0:T(8,128)} %get-tuple-element.49.lse_ref) | copy-start | bytes 589828
  215.5 1.5 copy-start.12
  216.2 5.1 %copy-start.9 = (bf16[2,1024,1152]{2,1,0:T(8,128)(2,1)}, bf16[2,1024,1152]{2,1,0:T(8,128)(2,1)S(1)}, u32[]{:S(2)}) copy-start(bf16[2,1024,1152]{2,1,0:T(8,128)(2,1)S(1)} %constant_dynamic-update-slice_fusion) | copy-start | bytes 14155780
  221.3 3.1 copy-start.2
  222.8 11.1 %collective-permute-start.1 = (bf16[2,512,768]{2,1,0:T(8,128)(2,1)}, bf16[2,512,768]{2,1,0:T(8,128)(2,1)S(1)}, u32[]{:S(2)}, u32[]{:S(2)}) collective-permute-start(bf16[2,512,768]{2,1,0:T(8,128)(2,1)} %dynamic-slice_convert_fusion), channel_id=1, source_target_pairs={{0,1},{1,0},{2,3},{3,2},{4,5},{5,4},{6,7},{7,6},{8,9},{9,8},{10,11... | collective-permute-start | bytes 4718600 | tf_op jit(solution)/shard_map/ppermute | solution.py:844
  225.0 8.9 %copy-start.3 = (f32[2,1024,768]{2,1,0:T(8,128)S(1)}, f32[2,1024,768]{2,1,0:T(8,128)}, u32[]{:S(2)}) copy-start(f32[2,1024,768]{2,1,0:T(8,128)} %copy-done.2) | copy-start | bytes 18874372
  355.1 4.7 %copy-start.7 = (f32[4,48,2304]{2,1,0:T(8,128)S(1)}, f32[4,48,2304]{2,1,0:T(8,128)}, u32[]{:S(2)}) copy-start(f32[4,48,2304]{2,1,0:T(8,128)} %get-tuple-element.60) | copy-start | bytes 5308420
  359.7 1.4 copy-start.8
  359.7 2.7 copy-start.6
  361.2 2.6 copy-start.5
